TPU v7x, 32 devices: a whole 2x2x4 slice. The times are simulated.
32 devices in a mesh: fsdp: 8 (over y, x, core), tp: 4 (over z).
Axes of the slice: x: 2, y: 2, z: 4, core: 2. Of those that a mesh axis runs over, the one named last changes fastest.
Arguments:
- inputs: bfloat16 [16384, 1024], P(('fsdp', 'tp')), may hold values from -6 to 6
- seq_lengths: int32 [8, 7], P('fsdp'), may hold values from 1 to 512, 2048 in all within a row
- qkv_w: bfloat16 [3, 1024, 1024], P(None, 'fsdp', 'tp'), may hold values from -0.1875 to 0.1875
- out_w: bfloat16 [1024, 1024], P('tp', 'fsdp'), may hold values from -1 to 1
- fc_w: bfloat16 [1024, 4096], P('fsdp', 'tp'), may hold values from -0.1875 to 0.1875
- proj_w: bfloat16 [4096, 1024], P('tp', 'fsdp'), may hold values from -0.125 to 0.125
- ln1_gain: bfloat16 [1024], P(('fsdp', 'tp')), may hold values from 0.099609375 to 1.8984375
- ln1_bias: bfloat16 [1024], P(('fsdp', 'tp')), may hold values from -1.1953125 to 1.1953125
- q_bias: bfloat16 [1024], P(('fsdp', 'tp')), may hold values from -3 to 3
- v_bias: bfloat16 [1024], P(('fsdp', 'tp')), may hold values from -0.29882812 to 0.29882812
- out_bias: bfloat16 [1024], P(('fsdp', 'tp')), may hold values from -1.796875 to 1.796875
- ln2_gain: bfloat16 [1024], P(('fsdp', 'tp')), may hold values from 0.099609375 to 1.8984375
- ln2_bias: bfloat16 [1024], P(('fsdp', 'tp')), may hold values from -1.1953125 to 1.1953125
- fc_bias: bfloat16 [4096], P(('fsdp', 'tp')), may hold values from -1.796875 to 1.796875
- proj_bias: bfloat16 [1024], P(('fsdp', 'tp')), may hold values from -1.796875 to 1.796875
- cotangent: bfloat16 [16384, 1024], P(('fsdp', 'tp')), may hold values from -6 to 6
Outputs:
- outputs: float32 [16384, 1024], P(('fsdp', 'tp'))
- dinputs: float32 [16384, 1024], P(('fsdp', 'tp'))
- dqkv_w: float32 [3, 1024, 1024], P(None, 'fsdp', 'tp')
- dout_w: float32 [1024, 1024], P('tp', 'fsdp')
- dfc_w: float32 [1024, 4096], P('fsdp', 'tp')
- dproj_w: float32 [4096, 1024], P('tp', 'fsdp')
- dln1_gain: float32 [1024], P(('fsdp', 'tp'))
- dln1_bias: float32 [1024], P(('fsdp', 'tp'))
- dq_bias: float32 [1024], P(('fsdp', 'tp'))
- dv_bias: float32 [1024], P(('fsdp', 'tp'))
- dout_bias: float32 [1024], P(('fsdp', 'tp'))
- dln2_gain: float32 [1024], P(('fsdp', 'tp'))
- dln2_bias: float32 [1024], P(('fsdp', 'tp'))
- dfc_bias: float32 [4096], P(('fsdp', 'tp'))
- dproj_bias: float32 [1024], P(('fsdp', 'tp'))
Inputs may be any that keep to these rules, and one draw needn't show every extreme that they name: `seq_lengths`: each row lists the lengths of the 7 sequences packed in order into the 2048 tokens of one packed row; they sum to 2048 and the longest is exactly 512.
All inputs are finite; a program needn't handle non-finite values.
Results may differ from a plain program's by a relative error of at most 0.014.
Values may be sent and summed in bfloat16 or wider, within the bound.
No kernel may reach another device: no remote copies, remote signals or barrier semaphores. Data moves between devices by JAX's collectives and lax.ppermute only.
A program may use at most 192 MiB of HBM per device.

v0:
```python
import jax
import jax.numpy as jnp
from jax import lax
import numpy as np
from jax.experimental import pallas as pl
from jax.experimental.pallas import tpu as pltpu
from jax.sharding import PartitionSpec as P

HD = 64
QT = 256
EPSILON = 1e-05
MASKED = -1e30
BF = jnp.bfloat16
F32 = jnp.float32


def layer_norm(values, gain, shift):
    center = jnp.mean(values, axis=-1, keepdims=True)
    offset = values - center
    spread = jnp.mean(offset * offset, axis=-1, keepdims=True)
    return offset * lax.rsqrt(spread + EPSILON) * gain + shift


def gelu(values):
    return jax.nn.gelu(values, approximate=True)


def exchange(item, axis, mask):
    size = lax.axis_size(axis)
    return lax.ppermute(item, axis, [(i, i ^ mask) for i in range(size)])


def exchange_by_core(item, even_mask, odd_mask):
    size = lax.axis_size("fsdp")
    pairs = [(i, i ^ (odd_mask if i % 2 else even_mask)) for i in range(size)]
    return lax.ppermute(item, "fsdp", pairs)


def rotate(item, step):
    size = lax.axis_size("tp")
    return lax.ppermute(item, "tp", [(i, (i + step) % size) for i in range(size)])


def step_masks():
    bits = [1 << b for b in range(1, lax.axis_size("fsdp").bit_length() - 1)]
    return list(zip(bits, bits[::-1]))


def slot_blocks():
    held = [(0, 0)]
    for even, odd in step_masks():
        held = held + [(a ^ even, b ^ odd) for a, b in held]
    held = held + [(b ^ 1, a ^ 1) for a, b in held]
    table = np.asarray(held, np.int32)
    mine = lax.axis_index("fsdp")
    return mine ^ jnp.where(mine % 2 == 0, table[:, 0], table[:, 1])


def rotations(part):
    return [rotate(part, k) for k in range(1, lax.axis_size("tp"))]


def assemble_tp(part, got):
    size = lax.axis_size("tp")
    mine = lax.axis_index("tp")
    return jnp.concatenate(
        [lax.select_n((mine - p) % size, part, *got) for p in range(size)], axis=-1
    )


def grow(held, got):
    return jnp.concatenate([held, got], axis=1)


def gather_raw(held, masks):
    for even, odd in masks[:-1]:
        held = grow(held, exchange_by_core(held, even, odd))
    return held, exchange_by_core(held, *masks[-1])


def add_low(left, right):
    return (left.astype(F32) + right.astype(F32)).astype(BF)


def split_add(left, right):
    half = left.shape[1] // 2
    return (
        add_low(left[:, :half], right[:, :half]),
        add_low(left[:, half:], right[:, half:]),
    )


def scatter_raw(keep, send, masks):
    for even, odd in masks[:-1]:
        keep, send = split_add(keep, exchange_by_core(send, even, odd))
    return keep, exchange_by_core(send, *masks[-1])


def core_swap(item):
    return exchange(item, "fsdp", 1)


def scatter_tp_raw(slab):
    size = lax.axis_size("tp")
    mine = lax.axis_index("tp")
    cols = slab.shape[-1] // size
    parts = [slab[:, :, p * cols : (p + 1) * cols] for p in range(size)]
    got = [rotate(lax.select_n((mine + k) % size, *parts), k) for k in range(1, size)]
    return [lax.select_n(mine, *parts), *got]


def total_tp(parts):
    total = parts[0].astype(F32)
    for part in parts[1:]:
        total = total + part.astype(F32)
    return total


def join(*items):
    return jax.tree.unflatten(
        jax.tree.structure(items), lax.optimization_barrier(tuple(jax.tree.leaves(items)))
    )


def pick(items, order):
    slot = jnp.arange(items.shape[0], dtype=jnp.int32)
    chosen = (order[:, None] == slot[None, :]).reshape(
        (items.shape[0],) * 2 + (1,) * (items.ndim - 1)
    )
    return jnp.sum(jnp.where(chosen, items[None], jnp.zeros_like(items)[None]), axis=1).astype(
        items.dtype
    )


def inverse(blocks):
    slot = jnp.arange(blocks.shape[0], dtype=jnp.int32)
    return jnp.sum(jnp.where(blocks[None, :] == slot[:, None], slot[None, :], 0), axis=1)


def reorder(values, blocks, back=False):
    rows, width = values.shape
    count = blocks.shape[0]
    lanes = width // count
    if lanes % 128:
        order = inverse(blocks) if back else blocks
        split = pick(values.reshape(rows, count, lanes).swapaxes(0, 1), order)
        return split.swapaxes(0, 1).reshape(rows, width)

    def body(table, source, target):
        for j in range(count):
            moved = pl.ds(pl.multiple_of(table[j] * lanes, lanes), lanes)
            plain = pl.ds(j * lanes, lanes)
            if back:
                target[:, moved] = source[:, plain]
            else:
                target[:, plain] = source[:, moved]

    tile = pl.BlockSpec((rows // 4, width), lambda i: (i, 0))
    return pl.pallas_call(
        body,
        grid=(4,),
        in_specs=[pl.BlockSpec(memory_space=pltpu.SMEM), tile],
        out_specs=tile,
        out_shape=jax.ShapeDtypeStruct(values.shape, values.dtype),
        name="reorder",
    )(blocks, values)


def gather_vectors(vectors, which, blocks):
    pack = jnp.concatenate(vectors)[None, None]
    size = lax.axis_size("tp")
    mine = lax.axis_index("tp")
    got = [pack] + [rotate(pack, k) for k in range(1, size)]
    pack = jnp.concatenate(
        [lax.select_n((mine - p) % size, *got) for p in range(size)], axis=1
    )
    where = lax.axis_index("fsdp")
    for b in range(lax.axis_size("fsdp").bit_length() - 1):
        other = exchange(pack, "fsdp", 1 << b)
        high = (where >> b) % 2 == 1
        pack = jnp.concatenate(
            [jnp.where(high, other, pack), jnp.where(high, pack, other)], axis=0
        )
    moved = pick(pack, blocks)
    out, at = [], 0
    for item, exchanged in zip(vectors, which):
        source = moved if exchanged else pack
        out.append(source[:, :, at : at + item.shape[0]].reshape(1, -1).astype(F32))
        at += item.shape[0]
    return out


def pack_vectors(vectors, which, blocks):
    count = lax.axis_size("fsdp")
    size = lax.axis_size("tp")
    packs = [
        jnp.concatenate(
            [v.reshape(count, size, -1) for v, m in zip(vectors, which) if m == kind], axis=2
        )
        for kind in (True, False)
    ]
    return jnp.concatenate([pick(packs[0], inverse(blocks)), packs[1]], axis=2)


def scatter_pack(pack, bits):
    where = lax.axis_index("fsdp")
    for b in bits:
        half = pack.shape[0] // 2
        high = (where >> b) % 2 == 1
        low_part, high_part = pack[:half], pack[half:]
        keep = jnp.where(high, high_part, low_part)
        send = jnp.where(high, low_part, high_part)
        pack = keep + exchange(send, "fsdp", 1 << b)
    return pack


def unpack_vectors(pack, lengths, which):
    mine = lax.axis_index("tp")
    size = lax.axis_size("tp")
    rows = [pack[0, p] for p in range(size)]
    total = lax.select_n(mine, *rows)
    for k in range(1, size):
        total = total + rotate(lax.select_n((mine + k) % size, *rows), k)
    out, at = {}, 0
    for kind in (True, False):
        for i, length in enumerate(lengths):
            if which[i] == kind:
                out[i] = total[at : at + length]
                at += length
    return [out[i] for i in range(len(lengths))]


def head_lanes(shape, head):
    lane = lax.broadcasted_iota(jnp.int32, shape, 1)
    return (lane >= head * HD) & (lane < (head + 1) * HD)


def nt(left, right):
    return lax.dot_general(left, right, (((1,), (1,)), ((), ())), preferred_element_type=F32)


def nn(left, right):
    return lax.dot_general(left, right, (((1,), (0,)), ((), ())), preferred_element_type=F32)


def allowed_keys(lo_row, start, keys, queries, rows):
    key = start + lax.broadcasted_iota(jnp.int32, (keys, queries), 0)
    query = rows + start + lax.broadcasted_iota(jnp.int32, (keys, queries), 1)
    return (key >= lo_row) & (key <= query)


def attend_forward(lo_ref, q_ref, k_ref, v_ref, *refs):
    ctx_ref, lse_ref = refs[-2:]
    rows = q_ref.shape[0]
    width = rows + QT
    value_t = v_ref[...].T
    for tile in range(rows // QT):
        start = tile * QT
        query = q_ref[pl.ds(start, QT), :] * jnp.asarray(HD**-0.5, BF)
        keys = k_ref[pl.ds(start, width), :]
        allowed = allowed_keys(lo_ref[:, start : start + QT], start, width, QT, rows)
        parts = []
        for head in range(2):
            query_h = jnp.where(head_lanes(query.shape, head), query, jnp.zeros_like(query))
            scores = jnp.where(allowed, nt(keys, query_h), MASKED)
            peak = jnp.max(scores, axis=0, keepdims=True)
            expo = jnp.exp(scores - peak)
            total = jnp.sum(expo, axis=0, keepdims=True)
            attend = (expo * (1.0 / total)).astype(BF)
            parts.append(
                nn(value_t[head * HD : (head + 1) * HD, start : start + width], attend)
            )
            lse_ref[0, head : head + 1, start : start + QT] = peak + jnp.log(total)
        ctx_ref[pl.ds(start, QT), :] = jnp.concatenate(parts, axis=0).T.astype(BF)


def attend_backward(lo_ref, q_ref, k_ref, v_ref, ctx_ref, lse_ref, grad_ref, *refs):
    out_ref, dk_acc, dv_acc = refs[-3:]
    rows = q_ref.shape[0]
    width = rows + QT
    scale = HD**-0.5
    dk_acc[...] = jnp.zeros_like(dk_acc)
    dv_acc[...] = jnp.zeros_like(dv_acc)
    key_t = k_ref[...].T
    for tile in range(rows // QT):
        start = tile * QT
        query = q_ref[pl.ds(start, QT), :] * jnp.asarray(scale, BF)
        grad = grad_ref[pl.ds(start, QT), :]
        keys = k_ref[pl.ds(start, width), :]
        values = v_ref[pl.ds(start, width), :]
        allowed = allowed_keys(lo_ref[:, start : start + QT], start, width, QT, rows)
        inner_t = (grad.astype(F32) * ctx_ref[pl.ds(start, QT), :].astype(F32)).T
        parts = []
        dk_sum, dv_sum = None, None
        for head in range(2):
            lanes = head_lanes(query.shape, head)
            query_h = jnp.where(lanes, query, jnp.zeros_like(query))
            grad_h = jnp.where(lanes, grad, jnp.zeros_like(grad))
            scores = jnp.where(allowed, nt(keys, query_h), MASKED)
            attend = jnp.exp(scores - lse_ref[0, head : head + 1, start : start + QT])
            inner = jnp.sum(inner_t[head * HD : (head + 1) * HD, :], axis=0, keepdims=True)
            dscores = (attend * (nt(values, grad_h) - inner)).astype(BF)
            dv_part = nn(attend.astype(BF), grad_h)
            dk_part = nn(dscores, query_h)
            dv_sum = dv_part if dv_sum is None else dv_sum + dv_part
            dk_sum = dk_part if dk_sum is None else dk_sum + dk_part
            parts.append(
                nn(key_t[head * HD : (head + 1) * HD, start : start + width], dscores) * scale
            )
        out_ref[0, pl.ds(rows + start, QT), :] = jnp.concatenate(parts, axis=0).T.astype(BF)
        dk_acc[pl.ds(start, width), :] += dk_sum
        dv_acc[pl.ds(start, width), :] += dv_sum
    out_ref[0, pl.ds(0, rows), :] = jnp.zeros((rows, out_ref.shape[2]), BF)
    out_ref[1] = dk_acc[...].astype(BF)
    out_ref[2] = dv_acc[...].astype(BF)


LANES = 2 * HD


def attention_specs(rows, base):
    def projected(kind, height, block):
        return pl.BlockSpec((None, height, LANES), lambda pair: (kind, block, pair + base))

    return [
        pl.BlockSpec((1, rows), lambda pair: (0, 0)),
        projected(0, rows, 1),
        projected(1, 2 * rows, 0),
        projected(2, 2 * rows, 0),
    ]


def attention_forward(lo, qkv, part=0, parts=1, into=()):
    rows, width = qkv.shape[1] // 2, qkv.shape[2]
    pairs = width // LANES // parts
    base = pairs * part
    return pl.pallas_call(
        attend_forward,
        grid=(pairs,),
        in_specs=attention_specs(rows, base)
        + [pl.BlockSpec(memory_space=pl.ANY) for _ in into],
        out_specs=[
            pl.BlockSpec((rows, LANES), lambda pair: (0, pair + base)),
            pl.BlockSpec((1, 2, rows), lambda pair: (pair + base, 0, 0)),
        ],
        out_shape=[
            jax.ShapeDtypeStruct((rows, width), BF),
            jax.ShapeDtypeStruct((width // LANES, 2, rows), F32),
        ],
        input_output_aliases={4 + i: i for i in range(len(into))},
        compiler_params=pltpu.CompilerParams(vmem_limit_bytes=40 * 2**20),
        name="attend_forward",
    )(lo, qkv, qkv, qkv, *into)


def attention_backward(lo, qkv, context, lse, dcontext, part=0, parts=1, into=()):
    rows, width = qkv.shape[1] // 2, qkv.shape[2]
    pairs = width // LANES // parts
    base = pairs * part
    tokens = pl.BlockSpec((rows, LANES), lambda pair: (0, pair + base))
    return pl.pallas_call(
        attend_backward,
        grid=(pairs,),
        in_specs=attention_specs(rows, base)
        + [tokens, pl.BlockSpec((1, 2, rows), lambda pair: (pair + base, 0, 0)), tokens]
        + [pl.BlockSpec(memory_space=pl.ANY) for _ in into],
        out_specs=pl.BlockSpec((3, 2 * rows, LANES), lambda pair: (0, 0, pair + base)),
        out_shape=jax.ShapeDtypeStruct(qkv.shape, BF),
        scratch_shapes=[
            pltpu.VMEM((2 * rows, LANES), F32),
            pltpu.VMEM((2 * rows, LANES), F32),
        ],
        input_output_aliases={7 + i: i for i in range(len(into))},
        compiler_params=pltpu.CompilerParams(vmem_limit_bytes=40 * 2**20),
        name="attend_backward",
    )(lo, qkv, qkv, qkv, context, lse, dcontext, *into)


def nn_pieces(x_ref, pieces):
    quarter = pieces[0].shape[0]
    weight = jnp.concatenate([piece[...] for piece in pieces], axis=0)
    return nn(x_ref[:, : 4 * quarter], weight)


def nt_pieces(grad, pieces):
    weight = jnp.concatenate([piece[...] for piece in pieces], axis=0)
    return nt(grad, weight)


def project_body(x_ref, *refs):
    pieces, shift_ref, out_ref = refs[:4], refs[4], refs[5]
    out_ref[...] = (nn_pieces(x_ref, pieces) + shift_ref[...]).astype(BF)


def project(x, pieces, shifts):
    rows, width = x.shape
    quarter, cols = pieces[0].shape[1:]
    tile = min(cols, 512)

    def part(height):
        return pl.BlockSpec((None, height, tile), lambda c, j: (c, 0, j))

    return pl.pallas_call(
        project_body,
        grid=(3, cols // tile),
        in_specs=[
            pl.BlockSpec((rows, width), lambda c, j: (0, 0)),
            *[part(quarter)] * 4,
            part(1),
        ],
        out_specs=part(rows),
        out_shape=jax.ShapeDtypeStruct((3, rows, cols), BF),
        compiler_params=pltpu.CompilerParams(vmem_limit_bytes=40 * 2**20),
        name="project",
    )(x, *pieces, shifts)


def project_back_body(grad_ref, *refs):
    pieces, (own_ref, send_ref, acc_ref) = refs[:4], refs[4:]
    kind = pl.program_id(0)
    rows = own_ref.shape[0]
    part = nt_pieces(grad_ref[...], pieces)

    @pl.when(kind == 0)
    def _():
        acc_ref[...] = part

    @pl.when(kind > 0)
    def _():
        acc_ref[...] += part

    @pl.when(kind == pl.num_programs(0) - 1)
    def _():
        send_ref[...] = acc_ref[:rows, :].astype(BF)
        own_ref[...] = acc_ref[rows:, :]


def project_back(grads, pieces):
    _, both, cols = grads.shape
    quarter = pieces[0].shape[1]
    rows = both // 2

    def part(height):
        return pl.BlockSpec((None, height, cols), lambda c: (c, 0, 0))

    whole = pl.BlockSpec((rows, 4 * quarter), lambda c: (0, 0))
    return pl.pallas_call(
        project_back_body,
        grid=(3,),
        in_specs=[part(both)] + [part(quarter)] * 4,
        out_specs=[whole, whole],
        out_shape=[
            jax.ShapeDtypeStruct((rows, 4 * quarter), F32),
            jax.ShapeDtypeStruct((rows, 4 * quarter), BF),
        ],
        scratch_shapes=[pltpu.VMEM((both, 4 * quarter), F32)],
        compiler_params=pltpu.CompilerParams(vmem_limit_bytes=40 * 2**20),
        name="project_back",
    )(grads, *pieces)


HIDDEN_TILE = 512
GELU_C = 0.7978845608028654
GELU_A = 0.044715


def up_body(x_ref, *refs):
    pieces, (shift_ref, hidden_ref, slope_ref) = refs[:4], refs[4:]
    v = nn_pieces(x_ref, pieces) + shift_ref[...]
    square = v * v
    t = jnp.tanh(GELU_C * v * (1.0 + GELU_A * square))
    gate = 0.5 * (1.0 + t)
    hidden_ref[...] = (v * gate).astype(BF)
    slope = gate + (0.5 * GELU_C) * v * (1.0 - t * t) * (1.0 + (3.0 * GELU_A) * square)
    slope_ref[...] = slope.astype(BF)


def down_body(x_ref, *refs):
    pieces, slope_ref, up_pieces = refs[:4], refs[4], refs[5:9]
    dpre_ref, sum_ref, dsecond_ref = refs[9:]
    v = nn_pieces(x_ref, pieces)
    dpre = (v * slope_ref[...].astype(F32)).astype(BF)
    dpre_ref[...] = dpre
    sum_ref[...] = jnp.sum(dpre.astype(F32), axis=0, keepdims=True)
    part = nt_pieces(dpre, up_pieces)

    @pl.when(pl.program_id(0) == 0)
    def _():
        dsecond_ref[...] = part

    @pl.when(pl.program_id(0) > 0)
    def _():
        dsecond_ref[...] += part


def hidden_tile(height):
    return pl.BlockSpec((height, HIDDEN_TILE), lambda j: (0, j))


def piece_tiles(pieces):
    return [
        pl.BlockSpec((None, piece.shape[1], HIDDEN_TILE), lambda j: (0, 0, j)) for piece in pieces
    ]


def mlp_up(x, pieces, shift):
    rows, width = x.shape
    hidden = shift.shape[1]
    return pl.pallas_call(
        up_body,
        grid=(hidden // HIDDEN_TILE,),
        in_specs=[pl.BlockSpec((rows, width), lambda j: (0, 0))]
        + piece_tiles(pieces)
        + [hidden_tile(1)],
        out_specs=[hidden_tile(rows), hidden_tile(rows)],
        out_shape=[jax.ShapeDtypeStruct((rows, hidden), BF)] * 2,
        compiler_params=pltpu.CompilerParams(vmem_limit_bytes=40 * 2**20),
        name="mlp_up",
    )(x, *pieces, shift)


def mlp_down(x, pieces, slope, up_pieces):
    rows, width = x.shape
    hidden = slope.shape[1]
    whole = pl.BlockSpec((rows, width), lambda j: (0, 0))
    return pl.pallas_call(
        down_body,
        grid=(hidden // HIDDEN_TILE,),
        in_specs=[whole] + piece_tiles(pieces) + [hidden_tile(rows)] + piece_tiles(up_pieces),
        out_specs=[hidden_tile(rows), hidden_tile(1), whole],
        out_shape=[
            jax.ShapeDtypeStruct((rows, hidden), BF),
            jax.ShapeDtypeStruct((1, hidden), F32),
            jax.ShapeDtypeStruct((rows, width), F32),
        ],
        compiler_params=pltpu.CompilerParams(vmem_limit_bytes=40 * 2**20),
        name="mlp_down",
    )(x, *pieces, slope, *up_pieces)


def grad_body(x_ref, y_ref, *refs):
    pieces, turned = refs[-5:-1], refs[-1]
    first = (pl.program_id(0) == 0) & (pl.program_id(1) == 0)

    @pl.when(first)
    def _():
        turned[...] = x_ref[...].T

    quarter = pieces[0].shape[0]
    y = y_ref[...]
    for i, piece in enumerate(pieces):
        piece[...] = nn(turned[i * quarter : (i + 1) * quarter, :], y).astype(BF)


def weight_grads(x, y, kinds=1, place=0, into=()):
    rows, width = x.shape
    count, _, cols = y.shape
    tile = 512
    piece = jax.ShapeDtypeStruct((kinds, width // 4, cols), BF)
    return pl.pallas_call(
        grad_body,
        grid=(count, cols // tile),
        in_specs=[
            pl.BlockSpec((rows, width), lambda c, j: (0, 0)),
            pl.BlockSpec((None, rows, tile), lambda c, j: (c, 0, j)),
        ]
        + [pl.BlockSpec(memory_space=pl.ANY) for _ in into],
        out_specs=[pl.BlockSpec((None, width // 4, tile), lambda c, j: (c + place, 0, j))] * 4,
        out_shape=[piece] * 4,
        scratch_shapes=[pltpu.VMEM((width, rows), BF)],
        input_output_aliases={2 + i: i for i in range(len(into))},
        compiler_params=pltpu.CompilerParams(vmem_limit_bytes=40 * 2**20),
        name="weight_grads",
    )(x, y, *into)


def out_body(table, x_ref, *refs):
    pieces, (middle_ref, shift_ref, out_ref, acc_ref) = refs[:4], refs[4:]
    step = pl.program_id(0)
    part = nt_pieces(x_ref[...], pieces)

    @pl.when(step == 0)
    def _():
        acc_ref[...] = part + middle_ref[...] + shift_ref[...]

    @pl.when(step > 0)
    def _():
        acc_ref[...] += part

    @pl.when(step == pl.num_programs(0) - 1)
    def _():
        lanes = out_ref.shape[1] // table.shape[0]
        for j in range(table.shape[0]):
            moved = pl.ds(pl.multiple_of(table[j] * lanes, lanes), lanes)
            out_ref[:, moved] = acc_ref[:, j * lanes : (j + 1) * lanes]


def mlp_out(hidden, pieces, middle, shift, blocks):
    rows, width = middle.shape
    moves = (width // blocks.shape[0]) % 128 == 0
    table = blocks if moves else jnp.zeros((1,), jnp.int32)
    whole = pl.BlockSpec((rows, width), lambda j: (0, 0))
    out = pl.pallas_call(
        out_body,
        grid=(hidden.shape[1] // HIDDEN_TILE,),
        in_specs=[pl.BlockSpec(memory_space=pltpu.SMEM), hidden_tile(rows)]
        + piece_tiles(pieces)
        + [whole, pl.BlockSpec((1, width), lambda j: (0, 0))],
        out_specs=whole,
        out_shape=jax.ShapeDtypeStruct((rows, width), F32),
        scratch_shapes=[pltpu.VMEM((rows, width), F32)],
        compiler_params=pltpu.CompilerParams(vmem_limit_bytes=40 * 2**20),
        name="mlp_out",
    )(table, hidden, *pieces, middle, shift)
    return out if moves else reorder(out, blocks, back=True)


def normalize_body(before_ref, own_ref, gain_ref, shift_ref, out_ref):
    for part, ref in enumerate((before_ref, own_ref)):
        values = layer_norm(ref[...].astype(F32), gain_ref[...], shift_ref[...])
        out_ref[part] = values.astype(BF)


def normalize_both(before, own, gain, shift):
    rows, width = own.shape
    tile = pl.BlockSpec((rows // 4, width), lambda i: (i, 0))
    vector = pl.BlockSpec((1, width), lambda i: (0, 0))
    out = pl.pallas_call(
        normalize_body,
        grid=(4,),
        in_specs=[tile, tile, vector, vector],
        out_specs=pl.BlockSpec((2, rows // 4, width), lambda i: (0, i, 0)),
        out_shape=jax.ShapeDtypeStruct((2, rows, width), BF),
        name="normalize",
    )(before, own, gain, shift)
    return out.reshape(2 * rows, width)


def lowest_keys(lengths, rows):
    count = lengths.shape[0]
    step = jnp.arange(count, dtype=jnp.int32)
    ends = jnp.sum(jnp.where(step[None, :] <= step[:, None], lengths[None, :], 0), axis=1)
    base = lax.axis_index("tp") * rows
    places = base + jnp.arange(rows, dtype=jnp.int32)
    begins = jnp.max(jnp.where(ends[:, None] <= places[None, :], ends[:, None], 0), axis=0)
    return (begins - base + rows).astype(jnp.int32)[None, :]


def per_device(
    inputs,
    seq_lengths,
    qkv_w,
    out_w,
    fc_w,
    proj_w,
    ln1_gain,
    ln1_bias,
    q_bias,
    v_bias,
    out_bias,
    ln2_gain,
    ln2_bias,
    fc_bias,
    proj_bias,
    cotangent,
):
    rows = inputs.shape[0]
    quarter = inputs.shape[1] // 4
    tp_size = lax.axis_size("tp")
    masks = step_masks()
    near, far = masks[:-1], masks[-1:]
    blocks = slot_blocks()
    exchanged = [True, True, False, False, True, True, True, False, True]
    shards = [v.shape[0] for v in (ln1_gain, ln1_bias, q_bias, v_bias, out_bias)]
    shards += [v.shape[0] for v in (ln2_gain, ln2_bias, fc_bias, proj_bias)]
    bits = list(range(lax.axis_size("fsdp").bit_length() - 1))[::-1]

    def dot_nt(left, right):
        return jnp.einsum("rj,ij->ri", left, right, preferred_element_type=F32)

    def wide_nt(left, pieces, kind=0):
        return jnp.concatenate([dot_nt(left, piece[kind]) for piece in pieces], axis=1)

    def dot_pieces(left, pieces, kind):
        return sum(
            jnp.dot(quarter_of(left, i), piece[kind], preferred_element_type=F32)
            for i, piece in enumerate(pieces)
        )

    def quarter_of(values, i):
        return values[:, i * quarter : (i + 1) * quarter]

    attn_part = jnp.concatenate([qkv_w, out_w.T[None]], axis=0)
    attn_got = rotations(attn_part)
    vectors = [ln1_gain, ln1_bias, q_bias, v_bias, out_bias]
    vectors += [ln2_gain, ln2_bias, fc_bias, proj_bias]
    inputs, attn_part, *vectors = join(inputs, attn_part, *vectors)
    own = reorder(inputs, blocks)
    before = lax.ppermute(own, "tp", [(i, i + 1) for i in range(tp_size - 1)])
    (
        gain_one,
        shift_one,
        query_shift,
        value_shift,
        attn_shift,
        gain_two,
        shift_two,
        hidden_shift,
        mlp_shift,
    ) = gather_vectors(vectors, exchanged, blocks)
    cot = reorder(cotangent, blocks)
    lo = lowest_keys(seq_lengths[0], rows)
    proj_part = proj_w.T[None]

    *attn_got, gain_one, before, own, cot, fc_part, proj_part = join(
        *attn_got, gain_one, before, own, cot, fc_w[None], proj_part
    )
    attn_held, attn_got = gather_raw(assemble_tp(attn_part, attn_got), near)
    fc_got = rotations(fc_part)

    attn_got, own, proj_part = join(attn_got, own, proj_part)
    attn_a, attn_b = gather_raw(grow(attn_held, attn_got), far)
    attn_c = core_swap(attn_a)
    first_both = normalize_both(before, own, gain_one, shift_one)

    attn_b, attn_c, *fc_got, proj_part, first_both = join(
        attn_b, attn_c, *fc_got, proj_part, first_both
    )
    attn_d = core_swap(attn_b)
    fc_slab = assemble_tp(fc_part, fc_got)

    attn_d, fc_slab, first_both = join(attn_d, fc_slab, first_both)
    attn = (attn_a, attn_b, attn_c, attn_d)
    fc_held, fc_step = gather_raw(fc_slab, near)
    shifts = jnp.stack([query_shift, jnp.zeros_like(query_shift), value_shift])
    qkv = project(first_both, attn, shifts)

    fc_step, qkv, proj_part = join(fc_step, qkv, proj_part)
    fc_a, fc_b = gather_raw(grow(fc_held, fc_step), far)
    fc_c = core_swap(fc_a)
    proj_got = rotations(proj_part)
    context, lse = attention_forward(lo, qkv)

    fc_b, fc_c, *proj_got, context = join(fc_b, fc_c, *proj_got, context)
    fc_d = core_swap(fc_b)
    proj_held, proj_step = gather_raw(assemble_tp(proj_part, proj_got), near)
    residual = own.astype(F32)
    middle = residual + wide_nt(context, attn, 3) + attn_shift
    second_f, pull_two = jax.vjp(layer_norm, middle, gain_two[0], shift_two[0])
    second = second_f.astype(BF)

    fc_d, proj_step, second = join(fc_d, proj_step, second)
    fc = (fc_a, fc_b, fc_c, fc_d)
    proj_a, proj_b = gather_raw(grow(proj_held, proj_step), far)
    proj_c = core_swap(proj_a)
    hidden, slope = mlp_up(second, fc, hidden_shift)

    proj_b, proj_c, hidden, slope, second = join(proj_b, proj_c, hidden, slope, second)
    proj_d = core_swap(proj_b)
    dproj = weight_grads(cot, hidden[None])
    dproj_got = [core_swap(dproj[3]), core_swap(dproj[2])]

    proj_d, *dproj_got, dproj = join(proj_d, *dproj_got, dproj)
    proj = (proj_a, proj_b, proj_c, proj_d)
    _, dproj_got[0] = scatter_raw(dproj[0], add_low(dproj[1], dproj_got[0]), far)
    dpre, dhidden_bias, dsecond = mlp_down(cot, proj, slope, fc)
    dfc = weight_grads(second, dpre[None])

    *dproj_got, dfc, dsecond = join(*dproj_got, dfc, dsecond)
    dfc_got = [core_swap(dfc[3]), core_swap(dfc[2])]
    dproj_keep = add_low(dproj[0], dproj_got[1])
    dproj_keep, dproj_got = scatter_raw(*split_add(dproj_keep, dproj_got[0]), near[::-1])
    dmiddle_norm, dgain_two, dshift_two = pull_two(dsecond)
    dmiddle = cot.astype(F32) + dmiddle_norm
    dattn = dmiddle.astype(BF)
    dcontext = dot_pieces(dattn, attn, 3).astype(BF)
    dout = weight_grads(dattn, context[None], kinds=4, place=3)

    dproj_got, dcontext, dout, dfc_got = join(dproj_got, dcontext, dout, dfc_got)
    _, dfc_got[0] = scatter_raw(dfc[0], add_low(dfc[1], dfc_got[0]), far)
    dproj_parts = scatter_tp_raw(add_low(dproj_keep, dproj_got))
    dqkv = attention_backward(lo, qkv, context, lse, dcontext)

    dfc_got, dproj_parts, dqkv = join(dfc_got, dproj_parts, dqkv)
    dfc_keep = add_low(dfc[0], dfc_got[1])
    dfc_keep, dfc_got = scatter_raw(*split_add(dfc_keep, dfc_got[0]), near[::-1])

    dattn_w = weight_grads(first_both, dqkv, kinds=4, into=tuple(dout))

    dfc_got, dattn_w, dqkv = join(dfc_got, dattn_w, dqkv)
    dattn_got = [core_swap(dattn_w[3]), core_swap(dattn_w[2])]
    dfc_parts = scatter_tp_raw(add_low(dfc_keep, dfc_got))
    dfirst_own, dfirst_send = project_back(dqkv, attn)

    dattn_got, dattn_w, dfirst_own, dfirst_send, hidden = join(
        dattn_got, dattn_w, dfirst_own, dfirst_send, hidden
    )
    _, dattn_got[0] = scatter_raw(dattn_w[0], add_low(dattn_w[1], dattn_got[0]), far)
    dfirst_after = lax.ppermute(dfirst_send, "tp", [(i + 1, i) for i in range(tp_size - 1)])
    outputs = mlp_out(hidden, proj, middle, mlp_shift, blocks)

    dattn_got, dfc_parts, dfirst_after, outputs, dfirst_own, dfirst_send, before = join(
        dattn_got, dfc_parts, dfirst_after, outputs, dfirst_own, dfirst_send, before
    )
    dattn_keep = add_low(dattn_w[0], dattn_got[1])
    dattn_keep, dattn_got = scatter_raw(*split_add(dattn_keep, dattn_got[0]), near[::-1])
    _, pull_one = jax.vjp(layer_norm, residual, gain_one[0], shift_one[0])
    dresidual, gain_own, shift_own = pull_one(dfirst_own + dfirst_after.astype(F32))
    vectors = pack_vectors(
        [
            gain_own,
            shift_own,
            jnp.sum(dqkv[0], axis=0, dtype=F32),
            jnp.sum(dqkv[2], axis=0, dtype=F32),
            jnp.sum(dattn, axis=0, dtype=F32),
            dgain_two,
            dshift_two,
            dhidden_bias[0],
            jnp.sum(cot, axis=0, dtype=F32),
        ],
        exchanged,
        blocks,
    )

    dattn_got, vectors, dresidual = join(dattn_got, vectors, dresidual)
    attn_parts = scatter_tp_raw(add_low(dattn_keep, dattn_got))
    vectors = scatter_pack(vectors, bits)
    dinputs = reorder(dmiddle + dresidual, blocks, back=True)
    vector_grads = unpack_vectors(vectors, shards, exchanged)
    attn_grad = total_tp(attn_parts)
    return (
        outputs,
        dinputs,
        attn_grad[:3],
        attn_grad[3].T,
        total_tp(dfc_parts)[0],
        total_tp(dproj_parts)[0].T,
        *vector_grads,
    )


def solution(mesh):
    vector = P(("fsdp", "tp"))
    tokens = P(("fsdp", "tp"), None)
    weights = (P(None, "fsdp", "tp"), P("tp", "fsdp"), P("fsdp", "tp"), P("tp", "fsdp"))
    return jax.shard_map(
        per_device,
        mesh=mesh,
        in_specs=(tokens, P("fsdp", None), *weights, *([vector] * 9), tokens),
        out_specs=(tokens, tokens, *weights, *([vector] * 9)),
        check_vma=False,
    )
```

profile of v0, /device:TPU:0, one launch (start us, length us, event | category | flops | bytes accessed | tf_op | source)
XLA Modules:
  0.0 469.9 jit_solution(16828466576685943387)
XLA Ops:
  2.5 6.1 %concatenate.46 = bf16[384]{0:T(512)(128)(2,1)S(1)} concatenate(bf16[32]{0:T(256)(128)(2,1)} %param.24, bf16[32]{0:T(256)(128)(2,1)} %param.25, bf16[32]{0:T(256)(128)(2,1)} %param.26, bf16[32]{0:T(256)(128)(2,1)} %param.27, bf16[32]{0:T(256)(128)(2,1)} %param.28, bf16[32]{0:T(256)(128)(2,1)} %param.29, bf16[32]{0:T(256)(128)(2,1)} %param.30, bf16[128]{0:T(256)(128)(2,1)} %param.31, ...), dimensions={0} | concatenate | bytes 1536 | tf_op jit(solution)/shard_map/concatenate | solution.py:170
  39.9 18.5 %collective-permute-done.9.before_ref = bf16[512,1024]{1,0:T(8,128)(2,1)S(1)} collective-permute-done((bf16[512,1024]{1,0:T(8,128)(2,1)}, bf16[512,1024]{1,0:T(8,128)(2,1)S(1)}, u32[]{:S(2)}, u32[]{:S(2)}) %collective-permute-start.9) | collective-permute-done | bytes 1048608 | tf_op jit(solution)/shard_map/ppermute | solution.py:699
  60.9 13.3 %collective-permute-done.10 = bf16[4,128,1024]{2,1,0:T(8,128)(2,1)S(1)} collective-permute-done((bf16[4,128,1024]{2,1,0:T(8,128)(2,1)S(1)}, bf16[4,128,1024]{2,1,0:T(8,128)(2,1)S(1)}, u32[]{:S(2)}, u32[]{:S(2)}) %collective-permute-start.10) | collective-permute-done | bytes 1048608 | tf_op jit(solution)/shard_map/ppermute | solution.py:36
  76.0 6.8 %collective-permute-start.13 = (bf16[1,128,1024]{2,1,0:T(8,128)(2,1)}, bf16[1,128,1024]{2,1,0:T(8,128)(2,1)S(1)}, u32[]{:S(2)}, u32[]{:S(2)}) collective-permute-start(bf16[1,128,1024]{2,1,0:T(8,128)(2,1)} %bitcast.2), channel_id=1, source_target_pairs={{0,1},{1,2},{2,3},{3,0},{4,5},{5,6},{6,7},{7,4},{8,9},{9,10},{10,1... | collective-permute-start | bytes 786440 | tf_op jit(solution)/shard_map/ppermute | solution.py:41
  92.7 10.7 %collective-permute-done.14 = bf16[1,128,1024]{2,1,0:T(8,128)(2,1)S(1)} collective-permute-done((bf16[1,128,1024]{2,1,0:T(8,128)(2,1)}, bf16[1,128,1024]{2,1,0:T(8,128)(2,1)S(1)}, u32[]{:S(2)}, u32[]{:S(2)}) %collective-permute-start.14) | collective-permute-done | bytes 262176 | tf_op jit(solution)/shard_map/ppermute | solution.py:41
  114.0 10.1 %project.1.q_ref.k_ref.v_ref = bf16[3,1024,1024]{2,1,0:T(8,128)(2,1)} custom-call(bf16[1024,1024]{1,0:T(8,128)(2,1)S(1)} %bitcast.50, bf16[4,256,1024]{2,1,0:T(8,128)(2,1)S(1)} %pad_maximum_fusion.refs_0_, bf16[4,256,1024]{2,1,0:T(8,128)(2,1)} %collective-permute-done.11.refs_1_, bf16[4,256,1024]{2,1,0:T(8,128)(2,1)} %collective-permute-done.12.refs_2_, ...), custom_call_target="tpu_custom_call" | custom-call | tf_op jit(solution)/shard_map/project/pallas_call | solution.py:403
  129.9 6.1 %collective-permute-start.20 = (bf16[1,128,1024]{2,1,0:T(8,128)(2,1)S(1)}, bf16[1,128,1024]{2,1,0:T(8,128)(2,1)S(1)}, u32[]{:S(2)}, u32[]{:S(2)}) collective-permute-start(bf16[1,128,1024]{2,1,0:T(8,128)(2,1)S(1)} %bitcast.59), channel_id=1, source_target_pairs={{0,1},{1,2},{2,3},{3,0},{4,5},{5,6},{6,7},{7,4},{8,9},{9,10},{10,1... | collective-permute-start | bytes 786440 | tf_op jit(solution)/shard_map/ppermute | solution.py:41
  143.4 24.7 %attend_forward.1 = (bf16[512,1024]{1,0:T(8,128)(2,1)S(1)}, f32[8,2,512]{2,1,0:T(2,128)S(1)}) custom-call(s32[1,512]{1,0:T(1,128)S(1)} %bitcast.56, bf16[3,1024,1024]{2,1,0:T(8,128)(2,1)S(1)} %copy-done, bf16[3,1024,1024]{2,1,0:T(8,128)(2,1)S(1)} %copy-done, bf16[3,1024,1024]{2,1,0:T(8,128)(2,1)S(1)} %copy-done), custom_call_target="tpu_custom_call" | custom-call | tf_op jit(solution)/shard_map/attend_forward/pallas_call | solution.py:337
  175.7 7.6 %collective-permute-done.24 = bf16[1,128,4096]{2,1,0:T(8,128)(2,1)S(1)} collective-permute-done((bf16[1,128,4096]{2,1,0:T(8,128)(2,1)S(1)}, bf16[1,128,4096]{2,1,0:T(8,128)(2,1)S(1)}, u32[]{:S(2)}, u32[]{:S(2)}) %collective-permute-start.24) | collective-permute-done | bytes 1048608 | tf_op jit(solution)/shard_map/ppermute | solution.py:36
  184.7 12.4 %mlp_up.1 = (bf16[512,4096]{1,0:T(8,128)(2,1)S(1)}, bf16[512,4096]{1,0:T(8,128)(2,1)}) custom-call(bf16[512,1024]{1,0:T(8,128)(2,1)S(1)} %add_convert_fusion.16.x_ref, bf16[1,256,4096]{2,1,0:T(8,128)(2,1)} %constant_dynamic-update-slice_fusion.refs_0_.refs_5_, bf16[1,256,4096]{2,1,0:T(8,128)(2,1)} %collective-permute-done.18.refs_1_.refs_6_, ...), custom_call_target="tpu_custom_call" | custom-call | tf_op jit(solution)/shard_map/mlp_up/pallas_call | solution.py:509
  197.0 12.7 %collective-permute-done.25.refs_1_ = bf16[1,256,4096]{2,1,0:T(8,128)(2,1)} collective-permute-done((bf16[1,256,4096]{2,1,0:T(8,128)(2,1)S(1)}, bf16[1,256,4096]{2,1,0:T(8,128)(2,1)}, u32[]{:S(2)}, u32[]{:S(2)}) %collective-permute-start.25) | collective-permute-done | bytes 2097184 | tf_op jit(solution)/shard_map/ppermute | solution.py:36
  211.1 6.9 %weight_grads.4 = (bf16[1,256,4096]{2,1,0:T(8,128)(2,1)S(1)}, bf16[1,256,4096]{2,1,0:T(8,128)(2,1)S(1)}, bf16[1,256,4096]{2,1,0:T(8,128)(2,1)S(1)}, bf16[1,256,4096]{2,1,0:T(8,128)(2,1)S(1)}) custom-call(bf16[512,1024]{1,0:T(8,128)(2,1)S(1)} %copy-done.2, bf16[1,512,4096]{2,1,0:T(8,128)(2,1)S(1)} %bitcast.52), custom_call_target="tpu_custom_call" | custom-call | tf_op jit(solution)/shard_map/weight_grads/pallas_call | solution.py:560
  231.5 14.7 %mlp_down.1 = (bf16[512,4096]{1,0:T(8,128)(2,1)}, f32[1,4096]{1,0:T(1,128)S(1)}, f32[512,1024]{1,0:T(8,128)S(1)}) custom-call(bf16[512,1024]{1,0:T(8,128)(2,1)S(1)} %copy-done.2, bf16[1,256,4096]{2,1,0:T(8,128)(2,1)S(1)} %pad_maximum_fusion.1.refs_0_, bf16[1,256,4096]{2,1,0:T(8,128)(2,1)} %collective-permute-done.25.refs_1_, ...), custom_call_target="tpu_custom_call" | custom-call | tf_op jit(solution)/shard_map/mlp_down/pallas_call | solution.py:526
  248.4 7.1 %weight_grads.5 = (bf16[1,256,4096]{2,1,0:T(8,128)(2,1)S(1)}, bf16[1,256,4096]{2,1,0:T(8,128)(2,1)S(1)}, bf16[1,256,4096]{2,1,0:T(8,128)(2,1)S(1)}, bf16[1,256,4096]{2,1,0:T(8,128)(2,1)S(1)}) custom-call(bf16[512,1024]{1,0:T(8,128)(2,1)S(1)} %add_convert_fusion.16.x_ref, bf16[1,512,4096]{2,1,0:T(8,128)(2,1)S(1)} %bitcast.53), custom_call_target="tpu_custom_call" | custom-call | tf_op jit(solution)/shard_map/weight_grads/pallas_call | solution.py:560
  288.2 21.7 %attend_backward.1.y_ref.grad_ref = bf16[3,1024,1024]{2,1,0:T(8,128)(2,1)S(1)} custom-call(s32[1,512]{1,0:T(1,128)S(1)} %bitcast.57, bf16[3,1024,1024]{2,1,0:T(8,128)(2,1)} %project.1.q_ref.k_ref.v_ref, bf16[3,1024,1024]{2,1,0:T(8,128)(2,1)} %project.1.q_ref.k_ref.v_ref, bf16[3,1024,1024]{2,1,0:T(8,128)(2,1)} %project.1.q_ref.k_ref.v_ref, ...), custom_call_target="tpu_custom_call" | custom-call | tf_op jit(solution)/shard_map/attend_backward/pallas_call | solution.py:361
  317.7 10.9 %weight_grads.7 = (bf16[4,256,1024]{2,1,0:T(8,128)(2,1)S(1)}, bf16[4,256,1024]{2,1,0:T(8,128)(2,1)S(1)}, bf16[4,256,1024]{2,1,0:T(8,128)(2,1)}, bf16[4,256,1024]{2,1,0:T(8,128)(2,1)}) custom-call(bf16[1024,1024]{1,0:T(8,128)(2,1)S(1)} %bitcast.51, ...), custom_call_target="tpu_custom_call", output_to_operand_aliasing={{0}: (2, {}), {1}: (3, {}), {2}: (4, {}), {3}: (5, {})} | custom-call | tf_op jit(solution)/shard_map/weight_grads/pallas_call | solution.py:560
  336.5 10.5 %project_back.1 = (f32[512,1024]{1,0:T(8,128)S(1)}, bf16[512,1024]{1,0:T(8,128)(2,1)S(1)}) custom-call(bf16[3,1024,1024]{2,1,0:T(8,128)(2,1)} %copy-done.1, bf16[4,256,1024]{2,1,0:T(8,128)(2,1)S(1)} %copy-done.4, bf16[4,256,1024]{2,1,0:T(8,128)(2,1)} %collective-permute-done.11.refs_1_, bf16[4,256,1024]{2,1,0:T(8,128)(2,1)} %collective-permute-done.12.refs_2_, ...), custom_call_target="tpu_custom_call" | custom-call | tf_op jit(solution)/shard_map/project_back/pallas_call | solution.py:447
  347.0 5.0 %add_convert_fusion.1 = bf16[4,256,1024]{2,1,0:T(8,128)(2,1)} fusion(bf16[4,256,1024]{2,1,0:T(8,128)(2,1)} %collective-permute-done.39, bf16[4,256,1024]{2,1,0:T(8,128)(2,1)S(1)} %copy-done.23), kind=kLoop, calls=%fused_computation.3 | loop fusion | flops 4194304 | bytes 6291456 | tf_op jit(solution)/shard_map/convert_element_type | solution.py:82
  376.9 11.4 %mlp_out.1 = f32[512,1024]{1,0:T(8,128)} custom-call(s32[8]{0:T(128)S(1)} %copy-done.40, bf16[512,4096]{1,0:T(8,128)(2,1)} %copy-done.9, bf16[1,256,4096]{2,1,0:T(8,128)(2,1)S(1)} %copy-done.8, bf16[1,256,4096]{2,1,0:T(8,128)(2,1)} %collective-permute-done.25.refs_1_, bf16[1,256,4096]{2,1,0:T(8,128)(2,1)S(1)} %copy-done.27, ...), custom_call_target="tpu_custom_call" | custom-call | tf_op jit(solution)/shard_map/mlp_out/pallas_call | solution.py:603
  388.3 4.6 collective-permute-done.42
  392.9 9.7 %collective-permute-done.43 = bf16[1,128,1024]{2,1,0:T(8,128)(2,1)} collective-permute-done((bf16[1,128,1024]{2,1,0:T(8,128)(2,1)}, bf16[1,128,1024]{2,1,0:T(8,128)(2,1)}, u32[]{:S(2)}, u32[]{:S(2)}) %collective-permute-start.43) | collective-permute-done | bytes 262176 | tf_op jit(solution)/shard_map/ppermute | solution.py:41
  432.8 6.5 %collective-permute-start.54 = (f32[384]{0:T(512)S(1)}, f32[384]{0:T(512)S(1)}, u32[]{:S(2)}, u32[]{:S(2)}) collective-permute-start(f32[384]{0:T(512)S(1)} %get-tuple-element.324), channel_id=1, source_target_pairs={{0,2},{1,3},{2,0},{3,1},{4,6},{5,7},{6,4},{7,5},{8,10},{9,11},{10,... | collective-permute-start | bytes 4616 | tf_op jit(solution)/shard_map/ppermute | solution.py:41
  448.8 5.1 %collective-permute-done.49 = bf16[4,128,256]{2,1,0:T(8,128)(2,1)S(1)} collective-permute-done((bf16[4,128,256]{2,1,0:T(8,128)(2,1)S(1)}, bf16[4,128,256]{2,1,0:T(8,128)(2,1)S(1)}, u32[]{:S(2)}, u32[]{:S(2)}) %collective-permute-start.49) | collective-permute-done | bytes 262176 | tf_op jit(solution)/shard_map/ppermute | solution.py:41
  453.9 14.0 %collective-permute-done.48 = bf16[4,128,256]{2,1,0:T(8,128)(2,1)S(1)} collective-permute-done((bf16[4,128,256]{2,1,0:T(8,128)(2,1)S(1)}, bf16[4,128,256]{2,1,0:T(8,128)(2,1)S(1)}, u32[]{:S(2)}, u32[]{:S(2)}) %collective-permute-start.48) | collective-permute-done | bytes 262176 | tf_op jit(solution)/shard_map/ppermute | solution.py:41
  (363 shorter events, 211.0 us)
Async XLA Ops:
  18.1 21.8 %collective-permute-start.1 = (bf16[4,128,256]{2,1,0:T(8,128)(2,1)S(1)}, bf16[4,128,256]{2,1,0:T(8,128)(2,1)S(1)}, u32[]{:S(2)}, u32[]{:S(2)}) collective-permute-start(bf16[4,128,256]{2,1,0:T(8,128)(2,1)S(1)} %pad_maximum_fusion.5), channel_id=1, source_target_pairs={{0,2},{1,3},{2,0},{3,1},{4,6},{5,7},{6,4},{7,5},{8,10},{9,11},{10,... | collective-permute-start | bytes 786440 | tf_op jit(solution)/shard_map/ppermute | solution.py:41
  28.2 30.2 %collective-permute-start.9 = (bf16[512,1024]{1,0:T(8,128)(2,1)}, bf16[512,1024]{1,0:T(8,128)(2,1)S(1)}, u32[]{:S(2)}, u32[]{:S(2)}) collective-permute-start(bf16[512,1024]{1,0:T(8,128)(2,1)} %reorder.3.own_ref), channel_id=1, source_target_pairs={{0,1},{1,2},{2,3},{4,5},{5,6},{6,7},{8,9},{9,10},{10,11},{12,13},{... | collective-permute-start | bytes 3145736 | tf_op jit(solution)/shard_map/ppermute | solution.py:699
  74.4 29.0 %collective-permute-start.11 = (bf16[4,256,1024]{2,1,0:T(8,128)(2,1)S(1)}, bf16[4,256,1024]{2,1,0:T(8,128)(2,1)}, u32[]{:S(2)}, u32[]{:S(2)}) collective-permute-start(bf16[4,256,1024]{2,1,0:T(8,128)(2,1)S(1)} %pad_maximum_fusion.refs_0_), channel_id=1, source_target_pairs={{0,16},{4,12},{8,24},{12,4},{16,0},{20,28},{24,8},{28,20},{1,17},{... | collective-permute-start | bytes 6291464 | tf_op jit(solution)/shard_map/ppermute | solution.py:36
  76.0 27.4 %collective-permute-start.12 = (bf16[4,256,1024]{2,1,0:T(8,128)(2,1)S(1)}, bf16[4,256,1024]{2,1,0:T(8,128)(2,1)}, u32[]{:S(2)}, u32[]{:S(2)}) collective-permute-start(bf16[4,256,1024]{2,1,0:T(8,128)(2,1)S(1)} %pad_maximum_fusion.refs_0_), channel_id=1, source_target_pairs={{0,4},{4,0},{8,12},{12,8},{16,20},{20,16},{24,28},{28,24},{1,5},{5... | collective-permute-start | bytes 6291464 | tf_op jit(solution)/shard_map/ppermute | solution.py:30
  82.8 20.6 %collective-permute-start.14 = (bf16[1,128,1024]{2,1,0:T(8,128)(2,1)}, bf16[1,128,1024]{2,1,0:T(8,128)(2,1)S(1)}, u32[]{:S(2)}, u32[]{:S(2)}) collective-permute-start(bf16[1,128,1024]{2,1,0:T(8,128)(2,1)} %bitcast.2), channel_id=1, source_target_pairs={{0,2},{1,3},{2,0},{3,1},{4,6},{5,7},{6,4},{7,5},{8,10},{9,11},{10,... | collective-permute-start | bytes 786440 | tf_op jit(solution)/shard_map/ppermute | solution.py:41
  128.9 39.2 %collective-permute-start.18 = (bf16[1,256,4096]{2,1,0:T(8,128)(2,1)}, bf16[1,256,4096]{2,1,0:T(8,128)(2,1)}, u32[]{:S(2)}, u32[]{:S(2)}) collective-permute-start(bf16[1,256,4096]{2,1,0:T(8,128)(2,1)} %constant_dynamic-update-slice_fusion.refs_0_.refs_5_), channel_id=1, source_target_pairs={{0,16},{4,12},{8,24},{12,4},{16,0},{20,28},{24,8},{28,20},{1,17},{... | collective-permute-start | bytes 6291464 | tf_op jit(solution)/shard_map/ppermute | solution.py:36
  129.4 38.7 %collective-permute-start.19 = (bf16[1,256,4096]{2,1,0:T(8,128)(2,1)}, bf16[1,256,4096]{2,1,0:T(8,128)(2,1)}, u32[]{:S(2)}, u32[]{:S(2)}) collective-permute-start(bf16[1,256,4096]{2,1,0:T(8,128)(2,1)} %constant_dynamic-update-slice_fusion.refs_0_.refs_5_), channel_id=1, source_target_pairs={{0,4},{4,0},{8,12},{12,8},{16,20},{20,16},{24,28},{28,24},{1,5},{5... | collective-permute-start | bytes 6291464 | tf_op jit(solution)/shard_map/ppermute | solution.py:30
  129.9 38.2 %collective-permute-start.20 = (bf16[1,128,1024]{2,1,0:T(8,128)(2,1)S(1)}, bf16[1,128,1024]{2,1,0:T(8,128)(2,1)S(1)}, u32[]{:S(2)}, u32[]{:S(2)}) collective-permute-start(bf16[1,128,1024]{2,1,0:T(8,128)(2,1)S(1)} %bitcast.59), channel_id=1, source_target_pairs={{0,1},{1,2},{2,3},{3,0},{4,5},{5,6},{6,7},{7,4},{8,9},{9,10},{10,1... | collective-permute-start | bytes 786440 | tf_op jit(solution)/shard_map/ppermute | solution.py:41
  136.0 32.1 %collective-permute-start.21 = (bf16[1,128,1024]{2,1,0:T(8,128)(2,1)S(1)}, bf16[1,128,1024]{2,1,0:T(8,128)(2,1)S(1)}, u32[]{:S(2)}, u32[]{:S(2)}) collective-permute-start(bf16[1,128,1024]{2,1,0:T(8,128)(2,1)S(1)} %bitcast.60), channel_id=1, source_target_pairs={{0,2},{1,3},{2,0},{3,1},{4,6},{5,7},{6,4},{7,5},{8,10},{9,11},{10,... | collective-permute-start | bytes 786440 | tf_op jit(solution)/shard_map/ppermute | solution.py:41
  139.3 28.9 %collective-permute-start.22 = (bf16[1,128,1024]{2,1,0:T(8,128)(2,1)S(1)}, bf16[1,128,1024]{2,1,0:T(8,128)(2,1)S(1)}, u32[]{:S(2)}, u32[]{:S(2)}) collective-permute-start(bf16[1,128,1024]{2,1,0:T(8,128)(2,1)S(1)} %bitcast.61), channel_id=1, source_target_pairs={{0,3},{1,0},{2,1},{3,2},{4,7},{5,4},{6,5},{7,6},{8,11},{9,8},{10,9... | collective-permute-start | bytes 786440 | tf_op jit(solution)/shard_map/ppermute | solution.py:41
  183.5 26.2 %collective-permute-start.25 = (bf16[1,256,4096]{2,1,0:T(8,128)(2,1)S(1)}, bf16[1,256,4096]{2,1,0:T(8,128)(2,1)}, u32[]{:S(2)}, u32[]{:S(2)}) collective-permute-start(bf16[1,256,4096]{2,1,0:T(8,128)(2,1)S(1)} %pad_maximum_fusion.1.refs_0_), channel_id=1, source_target_pairs={{0,16},{4,12},{8,24},{12,4},{16,0},{20,28},{24,8},{28,20},{1,17},{... | collective-permute-start | bytes 6291464 | tf_op jit(solution)/shard_map/ppermute | solution.py:36
  184.5 25.2 %collective-permute-start.26 = (bf16[1,256,4096]{2,1,0:T(8,128)(2,1)S(1)}, bf16[1,256,4096]{2,1,0:T(8,128)(2,1)S(1)}, u32[]{:S(2)}, u32[]{:S(2)}) collective-permute-start(bf16[1,256,4096]{2,1,0:T(8,128)(2,1)S(1)} %pad_maximum_fusion.1.refs_0_), channel_id=1, source_target_pairs={{0,4},{4,0},{8,12},{12,8},{16,20},{20,16},{24,28},{28,24},{1,5},{5... | collective-permute-start | bytes 6291464 | tf_op jit(solution)/shard_map/ppermute | solution.py:30
  228.9 26.6 %collective-permute-start.30 = (bf16[1,256,4096]{2,1,0:T(8,128)(2,1)}, bf16[1,256,4096]{2,1,0:T(8,128)(2,1)}, u32[]{:S(2)}, u32[]{:S(2)}) collective-permute-start(bf16[1,256,4096]{2,1,0:T(8,128)(2,1)} %add_convert_fusion.5), channel_id=1, source_target_pairs={{0,16},{4,12},{8,24},{12,4},{16,0},{20,28},{24,8},{28,20},{1,17},{... | collective-permute-start | bytes 6291464 | tf_op jit(solution)/shard_map/ppermute | solution.py:36
  280.7 29.3 %collective-permute-start.34 = (bf16[1,256,4096]{2,1,0:T(8,128)(2,1)}, bf16[1,256,4096]{2,1,0:T(8,128)(2,1)}, u32[]{:S(2)}, u32[]{:S(2)}) collective-permute-start(bf16[1,256,4096]{2,1,0:T(8,128)(2,1)} %add_convert_fusion.3), channel_id=1, source_target_pairs={{0,16},{4,12},{8,24},{12,4},{16,0},{20,28},{24,8},{28,20},{1,17},{... | collective-permute-start | bytes 6291464 | tf_op jit(solution)/shard_map/ppermute | solution.py:36
  284.2 25.7 %collective-permute-start.35 = (bf16[1,128,1024]{2,1,0:T(8,128)(2,1)S(1)}, bf16[1,128,1024]{2,1,0:T(8,128)(2,1)S(1)}, u32[]{:S(2)}, u32[]{:S(2)}) collective-permute-start(bf16[1,128,1024]{2,1,0:T(8,128)(2,1)S(1)} %get-tuple-element.345), channel_id=1, source_target_pairs={{0,1},{1,2},{2,3},{3,0},{4,5},{5,6},{6,7},{7,4},{8,9},{9,10},{10,1... | collective-permute-start | bytes 786440 | tf_op jit(solution)/shard_map/ppermute | solution.py:41
  285.7 24.3 %collective-permute-start.36 = (bf16[1,128,1024]{2,1,0:T(8,128)(2,1)S(1)}, bf16[1,128,1024]{2,1,0:T(8,128)(2,1)S(1)}, u32[]{:S(2)}, u32[]{:S(2)}) collective-permute-start(bf16[1,128,1024]{2,1,0:T(8,128)(2,1)S(1)} %get-tuple-element.344), channel_id=1, source_target_pairs={{0,2},{1,3},{2,0},{3,1},{4,6},{5,7},{6,4},{7,5},{8,10},{9,11},{10,... | collective-permute-start | bytes 786440 | tf_op jit(solution)/shard_map/ppermute | solution.py:41
  285.7 24.2 %collective-permute-start.37 = (bf16[1,128,1024]{2,1,0:T(8,128)(2,1)S(1)}, bf16[1,128,1024]{2,1,0:T(8,128)(2,1)S(1)}, u32[]{:S(2)}, u32[]{:S(2)}) collective-permute-start(bf16[1,128,1024]{2,1,0:T(8,128)(2,1)S(1)} %get-tuple-element.342), channel_id=1, source_target_pairs={{0,3},{1,0},{2,1},{3,2},{4,7},{5,4},{6,5},{7,6},{8,11},{9,8},{10,9... | collective-permute-start | bytes 786440 | tf_op jit(solution)/shard_map/ppermute | solution.py:41
  352.1 50.5 %collective-permute-start.41 = (bf16[4,256,1024]{2,1,0:T(8,128)(2,1)}, bf16[4,256,1024]{2,1,0:T(8,128)(2,1)}, u32[]{:S(2)}, u32[]{:S(2)}) collective-permute-start(bf16[4,256,1024]{2,1,0:T(8,128)(2,1)} %add_convert_fusion.1), channel_id=1, source_target_pairs={{0,16},{4,12},{8,24},{12,4},{16,0},{20,28},{24,8},{28,20},{1,17},{... | collective-permute-start | bytes 6291464 | tf_op jit(solution)/shard_map/ppermute | solution.py:36
  358.0 44.5 %collective-permute-start.45 = (bf16[512,1024]{1,0:T(8,128)(2,1)}, bf16[512,1024]{1,0:T(8,128)(2,1)}, u32[]{:S(2)}, u32[]{:S(2)}) collective-permute-start(bf16[512,1024]{1,0:T(8,128)(2,1)} %copy-done.41), channel_id=1, source_target_pairs={{1,0},{2,1},{3,2},{5,4},{6,5},{7,6},{9,8},{10,9},{11,10},{13,12},{... | collective-permute-start | bytes 3145736 | tf_op jit(solution)/shard_map/ppermute | solution.py:799
  362.5 30.4 %collective-permute-start.42 = (bf16[1,128,1024]{2,1,0:T(8,128)(2,1)}, bf16[1,128,1024]{2,1,0:T(8,128)(2,1)}, u32[]{:S(2)}, u32[]{:S(2)}) collective-permute-start(bf16[1,128,1024]{2,1,0:T(8,128)(2,1)} %get-tuple-element.341), channel_id=1, source_target_pairs={{0,1},{1,2},{2,3},{3,0},{4,5},{5,6},{6,7},{7,4},{8,9},{9,10},{10,1... | collective-permute-start | bytes 786440 | tf_op jit(solution)/shard_map/ppermute | solution.py:41
  365.1 37.4 %collective-permute-start.43 = (bf16[1,128,1024]{2,1,0:T(8,128)(2,1)}, bf16[1,128,1024]{2,1,0:T(8,128)(2,1)}, u32[]{:S(2)}, u32[]{:S(2)}) collective-permute-start(bf16[1,128,1024]{2,1,0:T(8,128)(2,1)} %get-tuple-element.340), channel_id=1, source_target_pairs={{0,2},{1,3},{2,0},{3,1},{4,6},{5,7},{6,4},{7,5},{8,10},{9,11},{10,... | collective-permute-start | bytes 786440 | tf_op jit(solution)/shard_map/ppermute | solution.py:41
  368.3 34.3 %collective-permute-start.44 = (bf16[1,128,1024]{2,1,0:T(8,128)(2,1)}, bf16[1,128,1024]{2,1,0:T(8,128)(2,1)}, u32[]{:S(2)}, u32[]{:S(2)}) collective-permute-start(bf16[1,128,1024]{2,1,0:T(8,128)(2,1)} %get-tuple-element.338), channel_id=1, source_target_pairs={{0,3},{1,0},{2,1},{3,2},{4,7},{5,4},{6,5},{7,6},{8,11},{9,8},{10,9... | collective-permute-start | bytes 786440 | tf_op jit(solution)/shard_map/ppermute | solution.py:41
  447.1 20.8 %collective-permute-start.48 = (bf16[4,128,256]{2,1,0:T(8,128)(2,1)S(1)}, bf16[4,128,256]{2,1,0:T(8,128)(2,1)S(1)}, u32[]{:S(2)}, u32[]{:S(2)}) collective-permute-start(bf16[4,128,256]{2,1,0:T(8,128)(2,1)S(1)} %get-tuple-element.335), channel_id=1, source_target_pairs={{0,2},{1,3},{2,0},{3,1},{4,6},{5,7},{6,4},{7,5},{8,10},{9,11},{10,... | collective-permute-start | bytes 786440 | tf_op jit(solution)/shard_map/ppermute | solution.py:41
  447.1 20.8 %collective-permute-start.47 = (bf16[4,128,256]{2,1,0:T(8,128)(2,1)S(1)}, bf16[4,128,256]{2,1,0:T(8,128)(2,1)S(1)}, u32[]{:S(2)}, u32[]{:S(2)}) collective-permute-start(bf16[4,128,256]{2,1,0:T(8,128)(2,1)S(1)} %get-tuple-element.334), channel_id=1, source_target_pairs={{0,1},{1,2},{2,3},{3,0},{4,5},{5,6},{6,7},{7,4},{8,9},{9,10},{10,1... | collective-permute-start | bytes 786440 | tf_op jit(solution)/shard_map/ppermute | solution.py:41
  (101 other events, 1136.3 us)
where the time goes:
time: 477 us; the launch traced here: 470 us
  Pallas kernels  148 us (31%)
  waiting for transfers between devices  118 us (25%)
  starting transfers between devices  76 us (16%)
  other arithmetic  64.3 us (13%)
  local copies, waits for them, and re-layouts  50.9 us (11%)
  matrix products  10.4 us (2%)
    ppermute x24, starting transfers between devices, rotate(): lax.ppermute(item, 'tp', [(i, (i + step) % size) for i in range(size)])  52.8 us
    ppermute x24, waiting for transfers between devices, rotate(): lax.ppermute(item, 'tp', [(i, (i + step) % size) for i in range(size)])  47.8 us
    ppermute x12, waiting for transfers between devices, exchange_by_core(): return lax.ppermute(item, 'fsdp', pairs)  40 us
    convert_element_type x12, other arithmetic, add_low(): return (left.astype(F32) + right.astype(F32)).astype(BF)  36.1 us
    unnamed x143, local copies, waits for them, and re-layouts  35.3 us
    pallas_call x4, Pallas kernels, weight_grads(): pl.pallas_call(grad_body, grid=(count, cols // tile), in_specs=[pl.BlockS...  27.7 us
    pallas_call x1, Pallas kernels, attention_forward(): pl.pallas_call(attend_forward, grid=(pairs,), in_specs=attention_specs(ro...  24.7 us
    pallas_call x1, Pallas kernels, attention_backward(): pl.pallas_call(attend_backward, grid=(pairs,), in_specs=attention_specs(r...  21.7 us
  transfers between devices with their start and end apart: 56, of which 21 were waited for; matrix products, arithmetic and copies ran while one was open for 12% of the time, Pallas kernels for 32%

commit v1 on v0

--- a/solution.py
+++ b/solution.py
@@ -10,6 +10,7 @@
 QT = 256
 EPSILON = 1e-05
 MASKED = -1e30
+VMEM = 40 * 2**20
 BF = jnp.bfloat16
 F32 = jnp.float32
 
@@ -75,6 +76,7 @@
 def gather_raw(held, masks):
     for even, odd in masks[:-1]:
         held = grow(held, exchange_by_core(held, even, odd))
+    held = lax.optimization_barrier(held)
     return held, exchange_by_core(held, *masks[-1])
 
 
@@ -166,14 +168,9 @@
     )(blocks, values)
 
 
-def gather_vectors(vectors, which, blocks):
-    pack = jnp.concatenate(vectors)[None, None]
-    size = lax.axis_size("tp")
-    mine = lax.axis_index("tp")
-    got = [pack] + [rotate(pack, k) for k in range(1, size)]
-    pack = jnp.concatenate(
-        [lax.select_n((mine - p) % size, *got) for p in range(size)], axis=1
-    )
+def gather_vectors_fsdp(vectors):
+    width = vectors[0].shape[0]
+    pack = jnp.concatenate([v.reshape(1, 1, -1, width) for v in vectors], axis=2)
     where = lax.axis_index("fsdp")
     for b in range(lax.axis_size("fsdp").bit_length() - 1):
         other = exchange(pack, "fsdp", 1 << b)
@@ -181,12 +178,23 @@
         pack = jnp.concatenate(
             [jnp.where(high, other, pack), jnp.where(high, pack, other)], axis=0
         )
+    return pack
+
+
+def spread_vectors(pack, got, lengths, which, blocks):
+    size = lax.axis_size("tp")
+    mine = lax.axis_index("tp")
+    width = pack.shape[3]
+    pack = jnp.concatenate(
+        [lax.select_n((mine - p) % size, pack, *got) for p in range(size)], axis=1
+    )
     moved = pick(pack, blocks)
     out, at = [], 0
-    for item, exchanged in zip(vectors, which):
+    for length, exchanged in zip(lengths, which):
         source = moved if exchanged else pack
-        out.append(source[:, :, at : at + item.shape[0]].reshape(1, -1).astype(F32))
-        at += item.shape[0]
+        count = length // width
+        out.append(source[:, :, at : at + count].reshape(1, -1).astype(F32))
+        at += count
     return out
 
 
@@ -266,9 +274,10 @@
             peak = jnp.max(scores, axis=0, keepdims=True)
             expo = jnp.exp(scores - peak)
             total = jnp.sum(expo, axis=0, keepdims=True)
-            attend = (expo * (1.0 / total)).astype(BF)
+            attend = expo.astype(BF)
             parts.append(
                 nn(value_t[head * HD : (head + 1) * HD, start : start + width], attend)
+                * (1.0 / total)
             )
             lse_ref[0, head : head + 1, start : start + QT] = peak + jnp.log(total)
         ctx_ref[pl.ds(start, QT), :] = jnp.concatenate(parts, axis=0).T.astype(BF)
@@ -348,7 +357,7 @@
             jax.ShapeDtypeStruct((width // LANES, 2, rows), F32),
         ],
         input_output_aliases={4 + i: i for i in range(len(into))},
-        compiler_params=pltpu.CompilerParams(vmem_limit_bytes=40 * 2**20),
+        compiler_params=pltpu.CompilerParams(vmem_limit_bytes=VMEM),
         name="attend_forward",
     )(lo, qkv, qkv, qkv, *into)
 
@@ -371,7 +380,7 @@
             pltpu.VMEM((2 * rows, LANES), F32),
         ],
         input_output_aliases={7 + i: i for i in range(len(into))},
-        compiler_params=pltpu.CompilerParams(vmem_limit_bytes=40 * 2**20),
+        compiler_params=pltpu.CompilerParams(vmem_limit_bytes=VMEM),
         name="attend_backward",
     )(lo, qkv, qkv, qkv, context, lse, dcontext, *into)
 
@@ -392,25 +401,27 @@
     out_ref[...] = (nn_pieces(x_ref, pieces) + shift_ref[...]).astype(BF)
 
 
-def project(x, pieces, shifts):
+def project(x, pieces, shifts, kind=0):
     rows, width = x.shape
     quarter, cols = pieces[0].shape[1:]
     tile = min(cols, 512)
 
-    def part(height):
-        return pl.BlockSpec((None, height, tile), lambda c, j: (c, 0, j))
+    kinds = shifts.shape[0]
+
+    def part(height, first=0):
+        return pl.BlockSpec((None, height, tile), lambda c, j: (c + first, 0, j))
 
     return pl.pallas_call(
         project_body,
-        grid=(3, cols // tile),
+        grid=(kinds, cols // tile),
         in_specs=[
             pl.BlockSpec((rows, width), lambda c, j: (0, 0)),
-            *[part(quarter)] * 4,
+            *[part(quarter, kind)] * 4,
             part(1),
         ],
         out_specs=part(rows),
-        out_shape=jax.ShapeDtypeStruct((3, rows, cols), BF),
-        compiler_params=pltpu.CompilerParams(vmem_limit_bytes=40 * 2**20),
+        out_shape=jax.ShapeDtypeStruct((kinds, rows, cols), BF),
+        compiler_params=pltpu.CompilerParams(vmem_limit_bytes=VMEM),
         name="project",
     )(x, *pieces, shifts)
 
@@ -454,7 +465,7 @@
             jax.ShapeDtypeStruct((rows, 4 * quarter), BF),
         ],
         scratch_shapes=[pltpu.VMEM((both, 4 * quarter), F32)],
-        compiler_params=pltpu.CompilerParams(vmem_limit_bytes=40 * 2**20),
+        compiler_params=pltpu.CompilerParams(vmem_limit_bytes=VMEM),
         name="project_back",
     )(grads, *pieces)
 
@@ -514,7 +525,7 @@
         + [hidden_tile(1)],
         out_specs=[hidden_tile(rows), hidden_tile(rows)],
         out_shape=[jax.ShapeDtypeStruct((rows, hidden), BF)] * 2,
-        compiler_params=pltpu.CompilerParams(vmem_limit_bytes=40 * 2**20),
+        compiler_params=pltpu.CompilerParams(vmem_limit_bytes=VMEM),
         name="mlp_up",
     )(x, *pieces, shift)
 
@@ -533,7 +544,7 @@
             jax.ShapeDtypeStruct((1, hidden), F32),
             jax.ShapeDtypeStruct((rows, width), F32),
         ],
-        compiler_params=pltpu.CompilerParams(vmem_limit_bytes=40 * 2**20),
+        compiler_params=pltpu.CompilerParams(vmem_limit_bytes=VMEM),
         name="mlp_down",
     )(x, *pieces, slope, *up_pieces)
 
@@ -569,7 +580,7 @@
         out_shape=[piece] * 4,
         scratch_shapes=[pltpu.VMEM((width, rows), BF)],
         input_output_aliases={2 + i: i for i in range(len(into))},
-        compiler_params=pltpu.CompilerParams(vmem_limit_bytes=40 * 2**20),
+        compiler_params=pltpu.CompilerParams(vmem_limit_bytes=VMEM),
         name="weight_grads",
     )(x, y, *into)
 
@@ -609,7 +620,7 @@
         out_specs=whole,
         out_shape=jax.ShapeDtypeStruct((rows, width), F32),
         scratch_shapes=[pltpu.VMEM((rows, width), F32)],
-        compiler_params=pltpu.CompilerParams(vmem_limit_bytes=40 * 2**20),
+        compiler_params=pltpu.CompilerParams(vmem_limit_bytes=VMEM),
         name="mlp_out",
     )(table, hidden, *pieces, middle, shift)
     return out if moves else reorder(out, blocks, back=True)
@@ -692,11 +703,24 @@
 
     attn_part = jnp.concatenate([qkv_w, out_w.T[None]], axis=0)
     attn_got = rotations(attn_part)
-    vectors = [ln1_gain, ln1_bias, q_bias, v_bias, out_bias]
-    vectors += [ln2_gain, ln2_bias, fc_bias, proj_bias]
-    inputs, attn_part, *vectors = join(inputs, attn_part, *vectors)
+    pack = gather_vectors_fsdp(
+        [ln1_gain, ln1_bias, q_bias, v_bias, out_bias, ln2_gain, ln2_bias, fc_bias, proj_bias]
+    )
     own = reorder(inputs, blocks)
+    cot = reorder(cotangent, blocks)
+    lo = lowest_keys(seq_lengths[0], rows)
+    proj_part = proj_w.T[None]
+
+    attn_got, pack, own, cot, fc_part, proj_part = join(
+        attn_got, pack, own, cot, fc_w[None], proj_part
+    )
+    attn_held, attn_got = gather_raw(assemble_tp(attn_part, attn_got), near)
+    pack_got = rotations(pack)
+
+    attn_got, pack_got, own = join(attn_got, pack_got, own)
     before = lax.ppermute(own, "tp", [(i, i + 1) for i in range(tp_size - 1)])
+    attn_a, attn_b = gather_raw(grow(attn_held, attn_got), far)
+    attn_c = core_swap(attn_a)
     (
         gain_one,
         shift_one,
@@ -707,62 +731,54 @@
         shift_two,
         hidden_shift,
         mlp_shift,
-    ) = gather_vectors(vectors, exchanged, blocks)
-    cot = reorder(cotangent, blocks)
-    lo = lowest_keys(seq_lengths[0], rows)
-    proj_part = proj_w.T[None]
-
-    *attn_got, gain_one, before, own, cot, fc_part, proj_part = join(
-        *attn_got, gain_one, before, own, cot, fc_w[None], proj_part
-    )
-    attn_held, attn_got = gather_raw(assemble_tp(attn_part, attn_got), near)
+    ) = spread_vectors(pack, pack_got, shards, exchanged, blocks)
+
+    attn_b, attn_c, before, gain_one, fc_part = join(attn_b, attn_c, before, gain_one, fc_part)
+    attn_d = core_swap(attn_b)
     fc_got = rotations(fc_part)
-
-    attn_got, own, proj_part = join(attn_got, own, proj_part)
-    attn_a, attn_b = gather_raw(grow(attn_held, attn_got), far)
-    attn_c = core_swap(attn_a)
     first_both = normalize_both(before, own, gain_one, shift_one)
 
-    attn_b, attn_c, *fc_got, proj_part, first_both = join(
-        attn_b, attn_c, *fc_got, proj_part, first_both
-    )
-    attn_d = core_swap(attn_b)
-    fc_slab = assemble_tp(fc_part, fc_got)
-
-    attn_d, fc_slab, first_both = join(attn_d, fc_slab, first_both)
+    attn_d, first_both = join(attn_d, first_both)
     attn = (attn_a, attn_b, attn_c, attn_d)
-    fc_held, fc_step = gather_raw(fc_slab, near)
     shifts = jnp.stack([query_shift, jnp.zeros_like(query_shift), value_shift])
     qkv = project(first_both, attn, shifts)
 
-    fc_step, qkv, proj_part = join(fc_step, qkv, proj_part)
+    fc_got, qkv = join(fc_got, qkv)
+    fc_held, fc_step = gather_raw(assemble_tp(fc_part, fc_got), near)
+    context, lse = attention_forward(lo, qkv, 0, 2)
+
+    fc_step, context, lse, proj_part = join(fc_step, context, lse, proj_part)
     fc_a, fc_b = gather_raw(grow(fc_held, fc_step), far)
     fc_c = core_swap(fc_a)
     proj_got = rotations(proj_part)
-    context, lse = attention_forward(lo, qkv)
-
-    fc_b, fc_c, *proj_got, context = join(fc_b, fc_c, *proj_got, context)
-    fc_d = core_swap(fc_b)
-    proj_held, proj_step = gather_raw(assemble_tp(proj_part, proj_got), near)
+    context, lse = attention_forward(lo, qkv, 1, 2, (context, lse))
     residual = own.astype(F32)
     middle = residual + wide_nt(context, attn, 3) + attn_shift
     second_f, pull_two = jax.vjp(layer_norm, middle, gain_two[0], shift_two[0])
     second = second_f.astype(BF)
 
-    fc_d, proj_step, second = join(fc_d, proj_step, second)
+    fc_b, fc_c, proj_got, second = join(fc_b, fc_c, proj_got, second)
+    fc_d = core_swap(fc_b)
+    proj_slab = assemble_tp(proj_part, proj_got)
+
+    fc_d, proj_slab, second = join(fc_d, proj_slab, second)
     fc = (fc_a, fc_b, fc_c, fc_d)
+    proj_held, proj_step = gather_raw(proj_slab, near)
+    hidden, slope = mlp_up(second, fc, hidden_shift)
+
+    proj_step, hidden, slope = join(proj_step, hidden, slope)
     proj_a, proj_b = gather_raw(grow(proj_held, proj_step), far)
     proj_c = core_swap(proj_a)
-    hidden, slope = mlp_up(second, fc, hidden_shift)
-
-    proj_b, proj_c, hidden, slope, second = join(proj_b, proj_c, hidden, slope, second)
-    proj_d = core_swap(proj_b)
     dproj = weight_grads(cot, hidden[None])
     dproj_got = [core_swap(dproj[3]), core_swap(dproj[2])]
 
-    proj_d, *dproj_got, dproj = join(proj_d, *dproj_got, dproj)
+    proj_b, proj_c, dproj_got, dproj = join(proj_b, proj_c, dproj_got, dproj)
+    proj_d = core_swap(proj_b)
+    dproj_send = add_low(dproj[1], dproj_got[0])
+
+    proj_d, dproj_send, second = join(proj_d, dproj_send, second)
     proj = (proj_a, proj_b, proj_c, proj_d)
-    _, dproj_got[0] = scatter_raw(dproj[0], add_low(dproj[1], dproj_got[0]), far)
+    _, dproj_got[0] = scatter_raw(dproj[0], dproj_send, far)
     dpre, dhidden_bias, dsecond = mlp_down(cot, proj, slope, fc)
     dfc = weight_grads(second, dpre[None])
 
@@ -773,7 +789,7 @@
     dmiddle_norm, dgain_two, dshift_two = pull_two(dsecond)
     dmiddle = cot.astype(F32) + dmiddle_norm
     dattn = dmiddle.astype(BF)
-    dcontext = dot_pieces(dattn, attn, 3).astype(BF)
+    dcontext = project(dattn, attn, jnp.zeros((1, 1, context.shape[1]), F32), 3)[0]
     dout = weight_grads(dattn, context[None], kinds=4, place=3)
 
     dproj_got, dcontext, dout, dfc_got = join(dproj_got, dcontext, dout, dfc_got)
@@ -792,15 +808,15 @@
     dfc_parts = scatter_tp_raw(add_low(dfc_keep, dfc_got))
     dfirst_own, dfirst_send = project_back(dqkv, attn)
 
-    dattn_got, dattn_w, dfirst_own, dfirst_send, hidden = join(
-        dattn_got, dattn_w, dfirst_own, dfirst_send, hidden
+    dattn_got, dattn_w, dfirst_own, dfirst_send, hidden, dfc_parts = join(
+        dattn_got, dattn_w, dfirst_own, dfirst_send, hidden, dfc_parts
     )
     _, dattn_got[0] = scatter_raw(dattn_w[0], add_low(dattn_w[1], dattn_got[0]), far)
     dfirst_after = lax.ppermute(dfirst_send, "tp", [(i + 1, i) for i in range(tp_size - 1)])
     outputs = mlp_out(hidden, proj, middle, mlp_shift, blocks)
 
-    dattn_got, dfc_parts, dfirst_after, outputs, dfirst_own, dfirst_send, before = join(
-        dattn_got, dfc_parts, dfirst_after, outputs, dfirst_own, dfirst_send, before
+    dattn_got, dfirst_after, outputs, dfirst_own = join(
+        dattn_got, dfirst_after, outputs, dfirst_own
     )
     dattn_keep = add_low(dattn_w[0], dattn_got[1])
     dattn_keep, dattn_got = scatter_raw(*split_add(dattn_keep, dattn_got[0]), near[::-1])
@@ -822,10 +838,16 @@
         blocks,
     )
 
-    dattn_got, vectors, dresidual = join(dattn_got, vectors, dresidual)
+    vectors = scatter_pack(vectors, bits)
+
+    dinputs = reorder(dmiddle + dresidual, blocks, back=True)
+    fc_grad = total_tp(dfc_parts)[0]
+    proj_grad = total_tp(dproj_parts)[0].T
+
+    dattn_got, vectors, dinputs, fc_grad, proj_grad = join(
+        dattn_got, vectors, dinputs, fc_grad, proj_grad
+    )
     attn_parts = scatter_tp_raw(add_low(dattn_keep, dattn_got))
-    vectors = scatter_pack(vectors, bits)
-    dinputs = reorder(dmiddle + dresidual, blocks, back=True)
     vector_grads = unpack_vectors(vectors, shards, exchanged)
     attn_grad = total_tp(attn_parts)
     return (
@@ -833,8 +855,8 @@
         dinputs,
         attn_grad[:3],
         attn_grad[3].T,
-        total_tp(dfc_parts)[0],
-        total_tp(dproj_parts)[0].T,
+        fc_grad,
+        proj_grad,
         *vector_grads,
     )
 

time: 477 us -> 446 us (0.935)
  waiting for transfers between devices: 118 us -> 100 us
  local copies, waits for them, and re-layouts: 50.9 us -> 39.6 us
  matrix products: 10.4 us -> 5.51 us
    ppermute x24, waiting for transfers between devices: 47.8 us -> 26.6 us  [rotate(): lax.ppermute(item, 'tp', [(i, (i + step) % size) for i in range(size)])]
    ppermute x12, waiting for transfers between devices: 40 us -> 26.6 us  [exchange_by_core(): return lax.ppermute(item, 'fsdp', pairs)]
    ppermute x1, waiting for transfers between devices: 0.01 us -> 7.92 us  [per_device(): lax.ppermute(dfirst_send, 'tp', [(i + 1, i) for i in range(tp_size - 1)])]
    ppermute x18, waiting for transfers between devices: 11.5 us -> 19.1 us  [exchange(): return lax.ppermute(item, axis, [(i, i ^ mask) for i in range(size)])]
    concatenate x3 -> x2, local copies, waits for them, and re-layouts: 8.42 us -> 1.61 us  [the longest x1 1.54 us: gather_vectors_fsdp(): jnp.concatenate([v.reshape(1, 1, -1, width) for v in vectors], axis=2)]
    convert_element_type x12, other arithmetic: 36.1 us -> 29.5 us  [add_low(): return (left.astype(F32) + right.astype(F32)).astype(BF)]
    dot_general x4 -> x0, matrix products: 6.29 us -> none  [dot_pieces(): jnp.dot(quarter_of(left, i), piece[kind], preferred_element_type=F32)]
    ppermute x24, starting transfers between devices: 52.8 us -> 47.6 us  [rotate(): lax.ppermute(item, 'tp', [(i, (i + step) % size) for i in range(size)])]
  transfers between devices with their start and end apart: 56 -> 56, of which waited for: 21 -> 16; matrix products, arithmetic and copies ran while one was open for 12% -> 10% of each run, Pallas kernels for 32% -> 34%
where the time goes in v1:
time: 446 us; the launch traced here: 438 us
  Pallas kernels  148 us (33%)
  waiting for transfers between devices  100 us (22%)
  starting transfers between devices  79.3 us (18%)
  other arithmetic  62.2 us (14%)
  local copies, waits for them, and re-layouts  39.6 us (9%)
  matrix products  5.51 us (1%)
    ppermute x24, starting transfers between devices, rotate(): lax.ppermute(item, 'tp', [(i, (i + step) % size) for i in range(size)])  47.6 us
    unnamed x188, local copies, waits for them, and re-layouts  32.6 us
    convert_element_type x12, other arithmetic, add_low(): return (left.astype(F32) + right.astype(F32)).astype(BF)  29.5 us
    pallas_call x4, Pallas kernels, weight_grads(): pl.pallas_call(grad_body, grid=(count, cols // tile), in_specs=[pl.BlockS...  26.8 us
    ppermute x24, waiting for transfers between devices, rotate(): lax.ppermute(item, 'tp', [(i, (i + step) % size) for i in range(size)])  26.6 us
    ppermute x12, waiting for transfers between devices, exchange_by_core(): return lax.ppermute(item, 'fsdp', pairs)  26.6 us
    pallas_call x1, Pallas kernels, attention_backward(): pl.pallas_call(attend_backward, grid=(pairs,), in_specs=attention_specs(r...  21.5 us
    pallas_call x2, Pallas kernels, attention_forward(): pl.pallas_call(attend_forward, grid=(pairs,), in_specs=attention_specs(ro...  21.2 us
  transfers between devices with their start and end apart: 56, of which 16 were waited for; matrix products, arithmetic and copies ran while one was open for 10% of the time, Pallas kernels for 34%

profile of v1, /device:TPU:0, one launch (start us, length us, event | category | flops | bytes accessed | tf_op | source)
XLA Modules:
  0.0 437.7 jit_solution(1369235843649574295)
XLA Ops:
  27.6 5.7 %collective-permute-start.7 = (bf16[8,1,12,32]{3,2,1,0:T(8,128)(2,1)S(1)}, bf16[8,1,12,32]{3,2,1,0:T(8,128)(2,1)S(1)}, u32[]{:S(2)}, u32[]{:S(2)}) collective-permute-start(bf16[8,1,12,32]{3,2,1,0:T(8,128)(2,1)S(1)} %pad_maximum_fusion.9), channel_id=1, source_target_pairs={{0,1},{1,2},{2,3},{3,0},{4,5},{5,6},{6,7},{7,4},{8,9},{9,10},{10,1... | collective-permute-start | bytes 18440 | tf_op jit(solution)/shard_map/ppermute | solution.py:42
  42.3 8.9 %collective-permute-start.12 = (bf16[512,1024]{1,0:T(8,128)(2,1)S(1)}, bf16[512,1024]{1,0:T(8,128)(2,1)}, u32[]{:S(2)}, u32[]{:S(2)}) collective-permute-start(bf16[512,1024]{1,0:T(8,128)(2,1)S(1)} %copy-done.53), channel_id=1, source_target_pairs={{0,1},{1,2},{2,3},{4,5},{5,6},{6,7},{8,9},{9,10},{10,11},{12,13},{... | collective-permute-start | bytes 3145736 | tf_op jit(solution)/shard_map/ppermute | solution.py:721
  53.2 20.2 %collective-permute-done.12.before_ref = bf16[512,1024]{1,0:T(8,128)(2,1)} collective-permute-done((bf16[512,1024]{1,0:T(8,128)(2,1)S(1)}, bf16[512,1024]{1,0:T(8,128)(2,1)}, u32[]{:S(2)}, u32[]{:S(2)}) %collective-permute-start.12) | collective-permute-done | bytes 1048608 | tf_op jit(solution)/shard_map/ppermute | solution.py:721
  79.6 4.5 %normalize.1 = bf16[2,512,1024]{2,1,0:T(8,128)(2,1)} custom-call(bf16[512,1024]{1,0:T(8,128)(2,1)} %collective-permute-done.12.before_ref, bf16[512,1024]{1,0:T(8,128)(2,1)} %reorder.3.own_ref, f32[1,1024]{1,0:T(1,128)} %reshape.380.gain_ref, f32[1,1024]{1,0:T(1,128)} %reshape.381.shift_ref), custom_call_target="tpu_custom_call" | custom-call | tf_op jit(solution)/shard_map/normalize/pallas_call | solution.py:639
  85.7 10.4 %project.2.q_ref.k_ref.v_ref = bf16[3,1024,1024]{2,1,0:T(8,128)(2,1)} custom-call(bf16[1024,1024]{1,0:T(8,128)(2,1)S(1)} %bitcast.50, bf16[4,256,1024]{2,1,0:T(8,128)(2,1)S(1)} %pad_maximum_fusion.refs_0_, bf16[4,256,1024]{2,1,0:T(8,128)(2,1)} %collective-permute-done.10.refs_1_, bf16[4,256,1024]{2,1,0:T(8,128)(2,1)} %collective-permute-done.11.refs_2_, ...), custom_call_target="tpu_custom_call" | custom-call | tf_op jit(solution)/shard_map/project/pallas_call | solution.py:414
  103.5 10.6 %attend_forward.2 = (bf16[512,1024]{1,0:T(8,128)(2,1)S(1)}, f32[8,2,512]{2,1,0:T(2,128)S(1)}) custom-call(s32[1,512]{1,0:T(1,128)S(1)} %bitcast.56, bf16[3,1024,1024]{2,1,0:T(8,128)(2,1)S(1)} %copy-done, bf16[3,1024,1024]{2,1,0:T(8,128)(2,1)S(1)} %copy-done, bf16[3,1024,1024]{2,1,0:T(8,128)(2,1)S(1)} %copy-done), custom_call_target="tpu_custom_call" | custom-call | tf_op jit(solution)/shard_map/attend_forward/pallas_call | solution.py:346
  116.4 5.6 %collective-permute-start.20 = (bf16[1,128,1024]{2,1,0:T(8,128)(2,1)S(1)}, bf16[1,128,1024]{2,1,0:T(8,128)(2,1)S(1)}, u32[]{:S(2)}, u32[]{:S(2)}) collective-permute-start(bf16[1,128,1024]{2,1,0:T(8,128)(2,1)S(1)} %bitcast.60), channel_id=1, source_target_pairs={{0,1},{1,2},{2,3},{3,0},{4,5},{5,6},{6,7},{7,4},{8,9},{9,10},{10,1... | collective-permute-start | bytes 786440 | tf_op jit(solution)/shard_map/ppermute | solution.py:42
  124.5 10.6 %attend_forward.3 = (bf16[512,1024]{1,0:T(8,128)(2,1)S(1)}, f32[8,2,512]{2,1,0:T(2,128)S(1)}) custom-call(s32[1,512]{1,0:T(1,128)S(1)} %bitcast.57, bf16[3,1024,1024]{2,1,0:T(8,128)(2,1)S(1)} %copy-done, bf16[3,1024,1024]{2,1,0:T(8,128)(2,1)S(1)} %copy-done, bf16[3,1024,1024]{2,1,0:T(8,128)(2,1)S(1)} %copy-done, ...), custom_call_target="tpu_custom_call", output_to_operand_aliasing={{0}: (4, {}), {1}: (5, {})} | custom-call | tf_op jit(solution)/shard_map/attend_forward/pallas_call | solution.py:346
  158.3 11.7 %mlp_up.1 = (bf16[512,4096]{1,0:T(8,128)(2,1)S(1)}, bf16[512,4096]{1,0:T(8,128)(2,1)}) custom-call(bf16[512,1024]{1,0:T(8,128)(2,1)S(1)} %add_convert_fusion.15.x_ref, bf16[1,256,4096]{2,1,0:T(8,128)(2,1)S(1)} %copy-done.9, bf16[1,256,4096]{2,1,0:T(8,128)(2,1)S(1)} %copy-done.29, bf16[1,256,4096]{2,1,0:T(8,128)(2,1)S(1)} %copy-done.31, ...), custom_call_target="tpu_custom_call" | custom-call | tf_op jit(solution)/shard_map/mlp_up/pallas_call | solution.py:520
  174.9 7.0 %weight_grads.4 = (bf16[1,256,4096]{2,1,0:T(8,128)(2,1)S(1)}, bf16[1,256,4096]{2,1,0:T(8,128)(2,1)S(1)}, bf16[1,256,4096]{2,1,0:T(8,128)(2,1)S(1)}, bf16[1,256,4096]{2,1,0:T(8,128)(2,1)S(1)}) custom-call(bf16[512,1024]{1,0:T(8,128)(2,1)S(1)} %copy-done.5, bf16[1,512,4096]{2,1,0:T(8,128)(2,1)S(1)} %bitcast.52), custom_call_target="tpu_custom_call" | custom-call | tf_op jit(solution)/shard_map/weight_grads/pallas_call | solution.py:571
  182.5 16.9 %collective-permute-done.25.refs_1_ = bf16[1,256,4096]{2,1,0:T(8,128)(2,1)S(1)} collective-permute-done((bf16[1,256,4096]{2,1,0:T(8,128)(2,1)S(1)}, bf16[1,256,4096]{2,1,0:T(8,128)(2,1)S(1)}, u32[]{:S(2)}, u32[]{:S(2)}) %collective-permute-start.25) | collective-permute-done | bytes 2097184 | tf_op jit(solution)/shard_map/ppermute | solution.py:37
  206.8 15.3 %mlp_down.1 = (bf16[512,4096]{1,0:T(8,128)(2,1)}, f32[1,4096]{1,0:T(1,128)S(1)}, f32[512,1024]{1,0:T(8,128)S(1)}) custom-call(bf16[512,1024]{1,0:T(8,128)(2,1)S(1)} %copy-done.5, bf16[1,256,4096]{2,1,0:T(8,128)(2,1)S(1)} %pad_maximum_fusion.2.refs_0_, bf16[1,256,4096]{2,1,0:T(8,128)(2,1)S(1)} %collective-permute-done.25.refs_1_, ...), custom_call_target="tpu_custom_call" | custom-call | tf_op jit(solution)/shard_map/mlp_down/pallas_call | solution.py:537
  224.2 7.9 %weight_grads.5 = (bf16[1,256,4096]{2,1,0:T(8,128)(2,1)S(1)}, bf16[1,256,4096]{2,1,0:T(8,128)(2,1)S(1)}, bf16[1,256,4096]{2,1,0:T(8,128)(2,1)}, bf16[1,256,4096]{2,1,0:T(8,128)(2,1)}) custom-call(bf16[512,1024]{1,0:T(8,128)(2,1)S(1)} %copy-done.15, bf16[1,512,4096]{2,1,0:T(8,128)(2,1)S(1)} %bitcast.55), custom_call_target="tpu_custom_call" | custom-call | tf_op jit(solution)/shard_map/weight_grads/pallas_call | solution.py:571
  250.8 4.8 %add_convert_fusion.3 = bf16[1,256,4096]{2,1,0:T(8,128)(2,1)} fusion(bf16[1,256,4096]{2,1,0:T(8,128)(2,1)} %collective-permute-done.32, bf16[1,256,4096]{2,1,0:T(8,128)(2,1)S(1)} %get-tuple-element.204), kind=kLoop, calls=%fused_computation.5 | loop fusion | flops 4194304 | bytes 6291456 | tf_op jit(solution)/shard_map/convert_element_type | solution.py:84
  258.8 5.0 %collective-permute-start.35 = (bf16[1,128,1024]{2,1,0:T(8,128)(2,1)S(1)}, bf16[1,128,1024]{2,1,0:T(8,128)(2,1)S(1)}, u32[]{:S(2)}, u32[]{:S(2)}) collective-permute-start(bf16[1,128,1024]{2,1,0:T(8,128)(2,1)S(1)} %get-tuple-element.350), channel_id=1, source_target_pairs={{0,1},{1,2},{2,3},{3,0},{4,5},{5,6},{6,7},{7,4},{8,9},{9,10},{10,1... | collective-permute-start | bytes 786440 | tf_op jit(solution)/shard_map/ppermute | solution.py:42
  266.4 21.5 %attend_backward.1.y_ref.grad_ref = bf16[3,1024,1024]{2,1,0:T(8,128)(2,1)S(1)} custom-call(s32[1,512]{1,0:T(1,128)S(1)} %bitcast.58, bf16[3,1024,1024]{2,1,0:T(8,128)(2,1)} %project.2.q_ref.k_ref.v_ref, bf16[3,1024,1024]{2,1,0:T(8,128)(2,1)} %project.2.q_ref.k_ref.v_ref, bf16[3,1024,1024]{2,1,0:T(8,128)(2,1)} %project.2.q_ref.k_ref.v_ref, ...), custom_call_target="tpu_custom_call" | custom-call | tf_op jit(solution)/shard_map/attend_backward/pallas_call | solution.py:370
  294.5 9.9 %weight_grads.7 = (bf16[4,256,1024]{2,1,0:T(8,128)(2,1)S(1)}, bf16[4,256,1024]{2,1,0:T(8,128)(2,1)S(1)}, bf16[4,256,1024]{2,1,0:T(8,128)(2,1)S(1)}, bf16[4,256,1024]{2,1,0:T(8,128)(2,1)S(1)}) custom-call(bf16[1024,1024]{1,0:T(8,128)(2,1)S(1)} %bitcast.51, ...), custom_call_target="tpu_custom_call", output_to_operand_aliasing={{0}: (2, {}), {1}: (3, {}), {2}: (4, {}), {3}: (5, {})} | custom-call | tf_op jit(solution)/shard_map/weight_grads/pallas_call | solution.py:571
  315.3 11.8 %project_back.1 = (f32[512,1024]{1,0:T(8,128)S(1)}, bf16[512,1024]{1,0:T(8,128)(2,1)}) custom-call(bf16[3,1024,1024]{2,1,0:T(8,128)(2,1)} %copy-done.1, bf16[4,256,1024]{2,1,0:T(8,128)(2,1)S(1)} %copy-done.4, bf16[4,256,1024]{2,1,0:T(8,128)(2,1)} %collective-permute-done.10.refs_1_, bf16[4,256,1024]{2,1,0:T(8,128)(2,1)} %collective-permute-done.11.refs_2_, ...), custom_call_target="tpu_custom_call" | custom-call | tf_op jit(solution)/shard_map/project_back/pallas_call | solution.py:458
  327.0 5.0 %collective-permute-done.42 = bf16[1,128,1024]{2,1,0:T(8,128)(2,1)S(1)} collective-permute-done((bf16[1,128,1024]{2,1,0:T(8,128)(2,1)S(1)}, bf16[1,128,1024]{2,1,0:T(8,128)(2,1)S(1)}, u32[]{:S(2)}, u32[]{:S(2)}) %collective-permute-start.42) | collective-permute-done | bytes 262176 | tf_op jit(solution)/shard_map/ppermute | solution.py:42
  332.1 4.9 %add_convert_fusion.1 = bf16[4,256,1024]{2,1,0:T(8,128)(2,1)} fusion(bf16[4,256,1024]{2,1,0:T(8,128)(2,1)} %collective-permute-done.39, bf16[4,256,1024]{2,1,0:T(8,128)(2,1)S(1)} %get-tuple-element.239), kind=kLoop, calls=%fused_computation.3 | loop fusion | flops 4194304 | bytes 6291456 | tf_op jit(solution)/shard_map/convert_element_type | solution.py:84
  350.3 11.2 %mlp_out.1 = f32[512,1024]{1,0:T(8,128)} custom-call(s32[8]{0:T(128)S(1)} %copy-done.52, bf16[512,4096]{1,0:T(8,128)(2,1)} %copy-done.13, bf16[1,256,4096]{2,1,0:T(8,128)(2,1)S(1)} %copy-done.12, bf16[1,256,4096]{2,1,0:T(8,128)(2,1)S(1)} %copy-done.35, bf16[1,256,4096]{2,1,0:T(8,128)(2,1)S(1)} %copy-done.38, bf16[1,256,4096]{2,1,0:T(8,128)(2,1)S(1)} %copy-done.40, ...), custom_call_target="tpu_custom_call" | custom-call | tf_op jit(solution)/shard_map/mlp_out/pallas_call | solution.py:614
  361.4 7.9 %collective-permute-done.45 = bf16[512,1024]{1,0:T(8,128)(2,1)} collective-permute-done((bf16[512,1024]{1,0:T(8,128)(2,1)}, bf16[512,1024]{1,0:T(8,128)(2,1)}, u32[]{:S(2)}, u32[]{:S(2)}) %collective-permute-start.45) | collective-permute-done | bytes 1048608 | tf_op jit(solution)/shard_map/ppermute | solution.py:815
  387.8 11.8 %collective-permute-done.48 = f32[2,4,384]{2,1,0:T(4,128)S(1)} collective-permute-done((f32[2,4,384]{2,1,0:T(4,128)S(1)}, f32[2,4,384]{2,1,0:T(4,128)S(1)}, u32[]{:S(2)}, u32[]{:S(2)}) %collective-permute-start.48) | collective-permute-done | bytes 12320 | tf_op jit(solution)/shard_map/ppermute | solution.py:31
  421.0 14.4 %collective-permute-done.51 = bf16[4,128,256]{2,1,0:T(8,128)(2,1)S(1)} collective-permute-done((bf16[4,128,256]{2,1,0:T(8,128)(2,1)S(1)}, bf16[4,128,256]{2,1,0:T(8,128)(2,1)S(1)}, u32[]{:S(2)}, u32[]{:S(2)}) %collective-permute-start.51) | collective-permute-done | bytes 262176 | tf_op jit(solution)/shard_map/ppermute | solution.py:42
  (406 shorter events, 191.6 us)
Async XLA Ops:
  2.5 23.1 %collective-permute-start = (bf16[4,128,256]{2,1,0:T(8,128)(2,1)S(1)}, bf16[4,128,256]{2,1,0:T(8,128)(2,1)S(1)}, u32[]{:S(2)}, u32[]{:S(2)}) collective-permute-start(bf16[4,128,256]{2,1,0:T(8,128)(2,1)S(1)} %pad_maximum_fusion.6), channel_id=1, source_target_pairs={{0,1},{1,2},{2,3},{3,0},{4,5},{5,6},{6,7},{7,4},{8,9},{9,10},{10,1... | collective-permute-start | bytes 786440 | tf_op jit(solution)/shard_map/ppermute | solution.py:42
  41.1 32.3 %collective-permute-start.10 = (bf16[4,256,1024]{2,1,0:T(8,128)(2,1)S(1)}, bf16[4,256,1024]{2,1,0:T(8,128)(2,1)}, u32[]{:S(2)}, u32[]{:S(2)}) collective-permute-start(bf16[4,256,1024]{2,1,0:T(8,128)(2,1)S(1)} %pad_maximum_fusion.refs_0_), channel_id=1, source_target_pairs={{0,16},{4,12},{8,24},{12,4},{16,0},{20,28},{24,8},{28,20},{1,17},{... | collective-permute-start | bytes 6291464 | tf_op jit(solution)/shard_map/ppermute | solution.py:37
  42.3 31.1 %collective-permute-start.11 = (bf16[4,256,1024]{2,1,0:T(8,128)(2,1)S(1)}, bf16[4,256,1024]{2,1,0:T(8,128)(2,1)}, u32[]{:S(2)}, u32[]{:S(2)}) collective-permute-start(bf16[4,256,1024]{2,1,0:T(8,128)(2,1)S(1)} %pad_maximum_fusion.refs_0_), channel_id=1, source_target_pairs={{0,4},{4,0},{8,12},{12,8},{16,20},{20,16},{24,28},{28,24},{1,5},{5... | collective-permute-start | bytes 6291464 | tf_op jit(solution)/shard_map/ppermute | solution.py:31
  42.3 31.1 %collective-permute-start.12 = (bf16[512,1024]{1,0:T(8,128)(2,1)S(1)}, bf16[512,1024]{1,0:T(8,128)(2,1)}, u32[]{:S(2)}, u32[]{:S(2)}) collective-permute-start(bf16[512,1024]{1,0:T(8,128)(2,1)S(1)} %copy-done.53), channel_id=1, source_target_pairs={{0,1},{1,2},{2,3},{4,5},{5,6},{6,7},{8,9},{9,10},{10,11},{12,13},{... | collective-permute-start | bytes 3145736 | tf_op jit(solution)/shard_map/ppermute | solution.py:721
  73.4 22.7 %collective-permute-start.13 = (bf16[1,128,1024]{2,1,0:T(8,128)(2,1)}, bf16[1,128,1024]{2,1,0:T(8,128)(2,1)}, u32[]{:S(2)}, u32[]{:S(2)}) collective-permute-start(bf16[1,128,1024]{2,1,0:T(8,128)(2,1)} %bitcast.67), channel_id=1, source_target_pairs={{0,1},{1,2},{2,3},{3,0},{4,5},{5,6},{6,7},{7,4},{8,9},{9,10},{10,1... | collective-permute-start | bytes 786440 | tf_op jit(solution)/shard_map/ppermute | solution.py:42
  115.9 26.4 %collective-permute-start.18 = (bf16[1,256,4096]{2,1,0:T(8,128)(2,1)S(1)}, bf16[1,256,4096]{2,1,0:T(8,128)(2,1)S(1)}, u32[]{:S(2)}, u32[]{:S(2)}) collective-permute-start(bf16[1,256,4096]{2,1,0:T(8,128)(2,1)S(1)} %pad_maximum_fusion.1.refs_0_.refs_5_), channel_id=1, source_target_pairs={{0,16},{4,12},{8,24},{12,4},{16,0},{20,28},{24,8},{28,20},{1,17},{... | collective-permute-start | bytes 6291464 | tf_op jit(solution)/shard_map/ppermute | solution.py:37
  116.4 25.9 %collective-permute-start.19 = (bf16[1,256,4096]{2,1,0:T(8,128)(2,1)S(1)}, bf16[1,256,4096]{2,1,0:T(8,128)(2,1)S(1)}, u32[]{:S(2)}, u32[]{:S(2)}) collective-permute-start(bf16[1,256,4096]{2,1,0:T(8,128)(2,1)S(1)} %pad_maximum_fusion.1.refs_0_.refs_5_), channel_id=1, source_target_pairs={{0,4},{4,0},{8,12},{12,8},{16,20},{20,16},{24,28},{28,24},{1,5},{5... | collective-permute-start | bytes 6291464 | tf_op jit(solution)/shard_map/ppermute | solution.py:31
  116.4 25.8 %collective-permute-start.20 = (bf16[1,128,1024]{2,1,0:T(8,128)(2,1)S(1)}, bf16[1,128,1024]{2,1,0:T(8,128)(2,1)S(1)}, u32[]{:S(2)}, u32[]{:S(2)}) collective-permute-start(bf16[1,128,1024]{2,1,0:T(8,128)(2,1)S(1)} %bitcast.60), channel_id=1, source_target_pairs={{0,1},{1,2},{2,3},{3,0},{4,5},{5,6},{6,7},{7,4},{8,9},{9,10},{10,1... | collective-permute-start | bytes 786440 | tf_op jit(solution)/shard_map/ppermute | solution.py:42
  122.0 20.3 %collective-permute-start.21 = (bf16[1,128,1024]{2,1,0:T(8,128)(2,1)S(1)}, bf16[1,128,1024]{2,1,0:T(8,128)(2,1)S(1)}, u32[]{:S(2)}, u32[]{:S(2)}) collective-permute-start(bf16[1,128,1024]{2,1,0:T(8,128)(2,1)S(1)} %bitcast.61), channel_id=1, source_target_pairs={{0,2},{1,3},{2,0},{3,1},{4,6},{5,7},{6,4},{7,5},{8,10},{9,11},{10,... | collective-permute-start | bytes 786440 | tf_op jit(solution)/shard_map/ppermute | solution.py:42
  149.9 20.1 %collective-permute-start.24 = (bf16[1,128,4096]{2,1,0:T(8,128)(2,1)}, bf16[1,128,4096]{2,1,0:T(8,128)(2,1)}, u32[]{:S(2)}, u32[]{:S(2)}) collective-permute-start(bf16[1,128,4096]{2,1,0:T(8,128)(2,1)} %pad_maximum_fusion.5), channel_id=1, source_target_pairs={{0,8},{4,20},{8,0},{12,28},{16,24},{20,4},{24,16},{28,12},{1,9},{5... | collective-permute-start | bytes 3145736 | tf_op jit(solution)/shard_map/ppermute | solution.py:37
  173.3 26.1 %collective-permute-start.25 = (bf16[1,256,4096]{2,1,0:T(8,128)(2,1)S(1)}, bf16[1,256,4096]{2,1,0:T(8,128)(2,1)S(1)}, u32[]{:S(2)}, u32[]{:S(2)}) collective-permute-start(bf16[1,256,4096]{2,1,0:T(8,128)(2,1)S(1)} %pad_maximum_fusion.2.refs_0_), channel_id=1, source_target_pairs={{0,16},{4,12},{8,24},{12,4},{16,0},{20,28},{24,8},{28,20},{1,17},{... | collective-permute-start | bytes 6291464 | tf_op jit(solution)/shard_map/ppermute | solution.py:37
  174.9 24.5 %collective-permute-start.26 = (bf16[1,256,4096]{2,1,0:T(8,128)(2,1)S(1)}, bf16[1,256,4096]{2,1,0:T(8,128)(2,1)S(1)}, u32[]{:S(2)}, u32[]{:S(2)}) collective-permute-start(bf16[1,256,4096]{2,1,0:T(8,128)(2,1)S(1)} %pad_maximum_fusion.2.refs_0_), channel_id=1, source_target_pairs={{0,4},{4,0},{8,12},{12,8},{16,20},{20,16},{24,28},{28,24},{1,5},{5... | collective-permute-start | bytes 6291464 | tf_op jit(solution)/shard_map/ppermute | solution.py:31
  203.7 28.5 %collective-permute-start.30 = (bf16[1,256,4096]{2,1,0:T(8,128)(2,1)}, bf16[1,256,4096]{2,1,0:T(8,128)(2,1)}, u32[]{:S(2)}, u32[]{:S(2)}) collective-permute-start(bf16[1,256,4096]{2,1,0:T(8,128)(2,1)} %add_convert_fusion.5), channel_id=1, source_target_pairs={{0,16},{4,12},{8,24},{12,4},{16,0},{20,28},{24,8},{28,20},{1,17},{... | collective-permute-start | bytes 6291464 | tf_op jit(solution)/shard_map/ppermute | solution.py:37
  255.6 32.4 %collective-permute-start.34 = (bf16[1,256,4096]{2,1,0:T(8,128)(2,1)}, bf16[1,256,4096]{2,1,0:T(8,128)(2,1)}, u32[]{:S(2)}, u32[]{:S(2)}) collective-permute-start(bf16[1,256,4096]{2,1,0:T(8,128)(2,1)} %add_convert_fusion.3), channel_id=1, source_target_pairs={{0,16},{4,12},{8,24},{12,4},{16,0},{20,28},{24,8},{28,20},{1,17},{... | collective-permute-start | bytes 6291464 | tf_op jit(solution)/shard_map/ppermute | solution.py:37
  258.8 29.1 %collective-permute-start.35 = (bf16[1,128,1024]{2,1,0:T(8,128)(2,1)S(1)}, bf16[1,128,1024]{2,1,0:T(8,128)(2,1)S(1)}, u32[]{:S(2)}, u32[]{:S(2)}) collective-permute-start(bf16[1,128,1024]{2,1,0:T(8,128)(2,1)S(1)} %get-tuple-element.350), channel_id=1, source_target_pairs={{0,1},{1,2},{2,3},{3,0},{4,5},{5,6},{6,7},{7,4},{8,9},{9,10},{10,1... | collective-permute-start | bytes 786440 | tf_op jit(solution)/shard_map/ppermute | solution.py:42
  263.8 24.2 %collective-permute-start.36 = (bf16[1,128,1024]{2,1,0:T(8,128)(2,1)S(1)}, bf16[1,128,1024]{2,1,0:T(8,128)(2,1)S(1)}, u32[]{:S(2)}, u32[]{:S(2)}) collective-permute-start(bf16[1,128,1024]{2,1,0:T(8,128)(2,1)S(1)} %get-tuple-element.349), channel_id=1, source_target_pairs={{0,2},{1,3},{2,0},{3,1},{4,6},{5,7},{6,4},{7,5},{8,10},{9,11},{10,... | collective-permute-start | bytes 786440 | tf_op jit(solution)/shard_map/ppermute | solution.py:42
  265.4 22.7 %collective-permute-start.37 = (bf16[1,128,1024]{2,1,0:T(8,128)(2,1)S(1)}, bf16[1,128,1024]{2,1,0:T(8,128)(2,1)S(1)}, u32[]{:S(2)}, u32[]{:S(2)}) collective-permute-start(bf16[1,128,1024]{2,1,0:T(8,128)(2,1)S(1)} %get-tuple-element.347), channel_id=1, source_target_pairs={{0,3},{1,0},{2,1},{3,2},{4,7},{5,4},{6,5},{7,6},{8,11},{9,8},{10,9... | collective-permute-start | bytes 786440 | tf_op jit(solution)/shard_map/ppermute | solution.py:42
  308.3 23.8 %collective-permute-start.39 = (bf16[4,256,1024]{2,1,0:T(8,128)(2,1)S(1)}, bf16[4,256,1024]{2,1,0:T(8,128)(2,1)}, u32[]{:S(2)}, u32[]{:S(2)}) collective-permute-start(bf16[4,256,1024]{2,1,0:T(8,128)(2,1)S(1)} %get-tuple-element.231), channel_id=1, source_target_pairs={{0,4},{4,0},{8,12},{12,8},{16,20},{20,16},{24,28},{28,24},{1,5},{5... | collective-permute-start | bytes 6291464 | tf_op jit(solution)/shard_map/ppermute | solution.py:31
  308.3 23.8 %collective-permute-start.40 = (bf16[4,256,1024]{2,1,0:T(8,128)(2,1)S(1)}, bf16[4,256,1024]{2,1,0:T(8,128)(2,1)S(1)}, u32[]{:S(2)}, u32[]{:S(2)}) collective-permute-start(bf16[4,256,1024]{2,1,0:T(8,128)(2,1)S(1)} %get-tuple-element.232), channel_id=1, source_target_pairs={{0,4},{4,0},{8,12},{12,8},{16,20},{20,16},{24,28},{28,24},{1,5},{5... | collective-permute-start | bytes 6291464 | tf_op jit(solution)/shard_map/ppermute | solution.py:31
  337.0 32.3 %collective-permute-start.44 = (bf16[4,256,1024]{2,1,0:T(8,128)(2,1)}, bf16[4,256,1024]{2,1,0:T(8,128)(2,1)}, u32[]{:S(2)}, u32[]{:S(2)}) collective-permute-start(bf16[4,256,1024]{2,1,0:T(8,128)(2,1)} %add_convert_fusion.1), channel_id=1, source_target_pairs={{0,16},{4,12},{8,24},{12,4},{16,0},{20,28},{24,8},{28,20},{1,17},{... | collective-permute-start | bytes 6291464 | tf_op jit(solution)/shard_map/ppermute | solution.py:37
  338.3 31.1 %collective-permute-start.45 = (bf16[512,1024]{1,0:T(8,128)(2,1)}, bf16[512,1024]{1,0:T(8,128)(2,1)}, u32[]{:S(2)}, u32[]{:S(2)}) collective-permute-start(bf16[512,1024]{1,0:T(8,128)(2,1)} %get-tuple-element.242), channel_id=1, source_target_pairs={{1,0},{2,1},{3,2},{5,4},{6,5},{7,6},{9,8},{10,9},{11,10},{13,12},{... | collective-permute-start | bytes 3145736 | tf_op jit(solution)/shard_map/ppermute | solution.py:815
  384.6 20.1 %collective-permute-start.46 = (bf16[4,128,1024]{2,1,0:T(8,128)(2,1)S(1)}, bf16[4,128,1024]{2,1,0:T(8,128)(2,1)}, u32[]{:S(2)}, u32[]{:S(2)}) collective-permute-start(bf16[4,128,1024]{2,1,0:T(8,128)(2,1)S(1)} %add_convert_fusion.8), channel_id=1, source_target_pairs={{0,8},{4,20},{8,0},{12,28},{16,24},{20,4},{24,16},{28,12},{1,9},{5... | collective-permute-start | bytes 3145736 | tf_op jit(solution)/shard_map/ppermute | solution.py:37
  414.2 21.2 %collective-permute-start.51 = (bf16[4,128,256]{2,1,0:T(8,128)(2,1)S(1)}, bf16[4,128,256]{2,1,0:T(8,128)(2,1)S(1)}, u32[]{:S(2)}, u32[]{:S(2)}) collective-permute-start(bf16[4,128,256]{2,1,0:T(8,128)(2,1)S(1)} %get-tuple-element.339), channel_id=1, source_target_pairs={{0,2},{1,3},{2,0},{3,1},{4,6},{5,7},{6,4},{7,5},{8,10},{9,11},{10,... | collective-permute-start | bytes 786440 | tf_op jit(solution)/shard_map/ppermute | solution.py:42
  415.2 20.2 %collective-permute-start.50 = (bf16[4,128,256]{2,1,0:T(8,128)(2,1)S(1)}, bf16[4,128,256]{2,1,0:T(8,128)(2,1)S(1)}, u32[]{:S(2)}, u32[]{:S(2)}) collective-permute-start(bf16[4,128,256]{2,1,0:T(8,128)(2,1)S(1)} %get-tuple-element.338), channel_id=1, source_target_pairs={{0,1},{1,2},{2,3},{3,0},{4,5},{5,6},{6,7},{7,4},{8,9},{9,10},{10,1... | collective-permute-start | bytes 786440 | tf_op jit(solution)/shard_map/ppermute | solution.py:42
  (124 other events, 1409.5 us)

commit v2 on v1

--- a/solution.py
+++ b/solution.py
@@ -198,16 +198,10 @@
     return out
 
 
-def pack_vectors(vectors, which, blocks):
+def pack_vectors(vectors):
     count = lax.axis_size("fsdp")
     size = lax.axis_size("tp")
-    packs = [
-        jnp.concatenate(
-            [v.reshape(count, size, -1) for v, m in zip(vectors, which) if m == kind], axis=2
-        )
-        for kind in (True, False)
-    ]
-    return jnp.concatenate([pick(packs[0], inverse(blocks)), packs[1]], axis=2)
+    return jnp.concatenate([v.reshape(count, size, -1) for v in vectors], axis=2)
 
 
 def scatter_pack(pack, bits):
@@ -222,20 +216,15 @@
     return pack
 
 
-def unpack_vectors(pack, lengths, which):
+def unpack_vectors(pack, lengths):
     mine = lax.axis_index("tp")
     size = lax.axis_size("tp")
     rows = [pack[0, p] for p in range(size)]
     total = lax.select_n(mine, *rows)
     for k in range(1, size):
         total = total + rotate(lax.select_n((mine + k) % size, *rows), k)
-    out, at = {}, 0
-    for kind in (True, False):
-        for i, length in enumerate(lengths):
-            if which[i] == kind:
-                out[i] = total[at : at + length]
-                at += length
-    return [out[i] for i in range(len(lengths))]
+    ends = np.cumsum(lengths)
+    return [total[end - length : end] for end, length in zip(ends, lengths)]
 
 
 def head_lanes(shape, head):
@@ -815,40 +804,41 @@
     dfirst_after = lax.ppermute(dfirst_send, "tp", [(i + 1, i) for i in range(tp_size - 1)])
     outputs = mlp_out(hidden, proj, middle, mlp_shift, blocks)
 
-    dattn_got, dfirst_after, outputs, dfirst_own = join(
-        dattn_got, dfirst_after, outputs, dfirst_own
+    proj_grad = total_tp(dproj_parts)[0].T
+    early = pack_vectors([jnp.sum(dattn, axis=0, dtype=F32), dgain_two, dshift_two])
+    early = jnp.concatenate(
+        [
+            pick(
+                jnp.concatenate([early, pack_vectors([jnp.sum(cot, axis=0, dtype=F32)])], axis=2),
+                inverse(blocks),
+            ),
+            pack_vectors([jnp.sum(dqkv[0], axis=0, dtype=F32)]),
+            pack_vectors([jnp.sum(dqkv[2], axis=0, dtype=F32), dhidden_bias[0]]),
+        ],
+        axis=2,
+    )
+
+    dattn_got, dfirst_after, outputs, dfirst_own, proj_grad, early = join(
+        dattn_got, dfirst_after, outputs, dfirst_own, proj_grad, early
     )
     dattn_keep = add_low(dattn_w[0], dattn_got[1])
     dattn_keep, dattn_got = scatter_raw(*split_add(dattn_keep, dattn_got[0]), near[::-1])
     _, pull_one = jax.vjp(layer_norm, residual, gain_one[0], shift_one[0])
     dresidual, gain_own, shift_own = pull_one(dfirst_own + dfirst_after.astype(F32))
-    vectors = pack_vectors(
-        [
-            gain_own,
-            shift_own,
-            jnp.sum(dqkv[0], axis=0, dtype=F32),
-            jnp.sum(dqkv[2], axis=0, dtype=F32),
-            jnp.sum(dattn, axis=0, dtype=F32),
-            dgain_two,
-            dshift_two,
-            dhidden_bias[0],
-            jnp.sum(cot, axis=0, dtype=F32),
-        ],
-        exchanged,
-        blocks,
-    )
-
+    late = pick(pack_vectors([gain_own, shift_own]), inverse(blocks))
+    vectors = jnp.concatenate([late, early], axis=2)
     vectors = scatter_pack(vectors, bits)
+    order = [0, 1, 4, 5, 6, 8, 2, 3, 7]
+    parts = unpack_vectors(vectors, [shards[i] for i in order])
+    vector_grads = [parts[order.index(i)] for i in range(len(order))]
 
     dinputs = reorder(dmiddle + dresidual, blocks, back=True)
+
+    dattn_got, vector_grads, dinputs, dfc_parts = join(
+        dattn_got, vector_grads, dinputs, dfc_parts
+    )
     fc_grad = total_tp(dfc_parts)[0]
-    proj_grad = total_tp(dproj_parts)[0].T
-
-    dattn_got, vectors, dinputs, fc_grad, proj_grad = join(
-        dattn_got, vectors, dinputs, fc_grad, proj_grad
-    )
     attn_parts = scatter_tp_raw(add_low(dattn_keep, dattn_got))
-    vector_grads = unpack_vectors(vectors, shards, exchanged)
     attn_grad = total_tp(attn_parts)
     return (
         outputs,

time: 446 us -> 443 us (level)
    ppermute x24, waiting for transfers between devices: 26.6 us -> 31.2 us  [rotate(): lax.ppermute(item, 'tp', [(i, (i + step) % size) for i in range(size)])]
    ppermute x18, waiting for transfers between devices: 19.1 us -> 14.5 us  [exchange(): return lax.ppermute(item, axis, [(i, i ^ mask) for i in range(size)])]
    unnamed x188 -> x170, local copies, waits for them, and re-layouts: 32.6 us -> 31.9 us
  transfers between devices with their start and end apart: 56 -> 56, of which waited for: 16 -> 18; matrix products, arithmetic and copies ran while one was open for 10% -> 11% of each run, Pallas kernels for 34% -> 34%
where the time goes in v2:
time: 443 us; the launch traced here: 435 us
  Pallas kernels  146 us (33%)
  waiting for transfers between devices  98.8 us (22%)
  starting transfers between devices  81.4 us (18%)
  other arithmetic  62.1 us (14%)
  local copies, waits for them, and re-layouts  38.7 us (9%)
  matrix products  5.5 us (1%)
    ppermute x24, starting transfers between devices, rotate(): lax.ppermute(item, 'tp', [(i, (i + step) % size) for i in range(size)])  47.6 us
    unnamed x170, local copies, waits for them, and re-layouts  31.9 us
    ppermute x24, waiting for transfers between devices, rotate(): lax.ppermute(item, 'tp', [(i, (i + step) % size) for i in range(size)])  31.2 us
    convert_element_type x12, other arithmetic, add_low(): return (left.astype(F32) + right.astype(F32)).astype(BF)  30 us
    pallas_call x4, Pallas kernels, weight_grads(): pl.pallas_call(grad_body, grid=(count, cols // tile), in_specs=[pl.BlockS...  26.8 us
    ppermute x12, waiting for transfers between devices, exchange_by_core(): return lax.ppermute(item, 'fsdp', pairs)  26.6 us
    pallas_call x1, Pallas kernels, attention_backward(): pl.pallas_call(attend_backward, grid=(pairs,), in_specs=attention_specs(r...  21.5 us
    pallas_call x2, Pallas kernels, attention_forward(): pl.pallas_call(attend_forward, grid=(pairs,), in_specs=attention_specs(ro...  21.2 us
  transfers between devices with their start and end apart: 56, of which 18 were waited for; matrix products, arithmetic and copies ran while one was open for 11% of the time, Pallas kernels for 34%

profile of v2, /device:TPU:0, one launch (start us, length us, event | category | flops | bytes accessed | tf_op | source)
XLA Modules:
  0.0 435.0 jit_solution(8798732992959153816)
XLA Ops:
  27.5 5.7 %collective-permute-start.7 = (bf16[8,1,12,32]{3,2,1,0:T(8,128)(2,1)S(1)}, bf16[8,1,12,32]{3,2,1,0:T(8,128)(2,1)S(1)}, u32[]{:S(2)}, u32[]{:S(2)}) collective-permute-start(bf16[8,1,12,32]{3,2,1,0:T(8,128)(2,1)S(1)} %pad_maximum_fusion.9), channel_id=1, source_target_pairs={{0,1},{1,2},{2,3},{3,0},{4,5},{5,6},{6,7},{7,4},{8,9},{9,10},{10,1... | collective-permute-start | bytes 18440 | tf_op jit(solution)/shard_map/ppermute | solution.py:42
  42.3 9.0 %collective-permute-start.12 = (bf16[512,1024]{1,0:T(8,128)(2,1)S(1)}, bf16[512,1024]{1,0:T(8,128)(2,1)}, u32[]{:S(2)}, u32[]{:S(2)}) collective-permute-start(bf16[512,1024]{1,0:T(8,128)(2,1)S(1)} %copy-done.53), channel_id=1, source_target_pairs={{0,1},{1,2},{2,3},{4,5},{5,6},{6,7},{8,9},{9,10},{10,11},{12,13},{... | collective-permute-start | bytes 3145736 | tf_op jit(solution)/shard_map/ppermute | solution.py:710
  53.1 20.2 %collective-permute-done.12.before_ref = bf16[512,1024]{1,0:T(8,128)(2,1)} collective-permute-done((bf16[512,1024]{1,0:T(8,128)(2,1)S(1)}, bf16[512,1024]{1,0:T(8,128)(2,1)}, u32[]{:S(2)}, u32[]{:S(2)}) %collective-permute-start.12) | collective-permute-done | bytes 1048608 | tf_op jit(solution)/shard_map/ppermute | solution.py:710
  79.5 4.5 %normalize.1 = bf16[2,512,1024]{2,1,0:T(8,128)(2,1)} custom-call(bf16[512,1024]{1,0:T(8,128)(2,1)} %collective-permute-done.12.before_ref, bf16[512,1024]{1,0:T(8,128)(2,1)} %reorder.3.own_ref, f32[1,1024]{1,0:T(1,128)} %reshape.382.gain_ref, f32[1,1024]{1,0:T(1,128)} %reshape.383.shift_ref), custom_call_target="tpu_custom_call" | custom-call | tf_op jit(solution)/shard_map/normalize/pallas_call | solution.py:628
  85.6 10.4 %project.2.q_ref.k_ref.v_ref = bf16[3,1024,1024]{2,1,0:T(8,128)(2,1)} custom-call(bf16[1024,1024]{1,0:T(8,128)(2,1)S(1)} %bitcast.50, bf16[4,256,1024]{2,1,0:T(8,128)(2,1)S(1)} %pad_maximum_fusion.refs_0_, bf16[4,256,1024]{2,1,0:T(8,128)(2,1)} %collective-permute-done.10.refs_1_, bf16[4,256,1024]{2,1,0:T(8,128)(2,1)} %collective-permute-done.11.refs_2_, ...), custom_call_target="tpu_custom_call" | custom-call | tf_op jit(solution)/shard_map/project/pallas_call | solution.py:403
  103.4 10.6 %attend_forward.2 = (bf16[512,1024]{1,0:T(8,128)(2,1)S(1)}, f32[8,2,512]{2,1,0:T(2,128)S(1)}) custom-call(s32[1,512]{1,0:T(1,128)S(1)} %bitcast.56, bf16[3,1024,1024]{2,1,0:T(8,128)(2,1)S(1)} %copy-done, bf16[3,1024,1024]{2,1,0:T(8,128)(2,1)S(1)} %copy-done, bf16[3,1024,1024]{2,1,0:T(8,128)(2,1)S(1)} %copy-done), custom_call_target="tpu_custom_call" | custom-call | tf_op jit(solution)/shard_map/attend_forward/pallas_call | solution.py:335
  116.3 5.6 %collective-permute-start.20 = (bf16[1,128,1024]{2,1,0:T(8,128)(2,1)S(1)}, bf16[1,128,1024]{2,1,0:T(8,128)(2,1)S(1)}, u32[]{:S(2)}, u32[]{:S(2)}) collective-permute-start(bf16[1,128,1024]{2,1,0:T(8,128)(2,1)S(1)} %bitcast.60), channel_id=1, source_target_pairs={{0,1},{1,2},{2,3},{3,0},{4,5},{5,6},{6,7},{7,4},{8,9},{9,10},{10,1... | collective-permute-start | bytes 786440 | tf_op jit(solution)/shard_map/ppermute | solution.py:42
  124.4 10.6 %attend_forward.3 = (bf16[512,1024]{1,0:T(8,128)(2,1)S(1)}, f32[8,2,512]{2,1,0:T(2,128)S(1)}) custom-call(s32[1,512]{1,0:T(1,128)S(1)} %bitcast.57, bf16[3,1024,1024]{2,1,0:T(8,128)(2,1)S(1)} %copy-done, bf16[3,1024,1024]{2,1,0:T(8,128)(2,1)S(1)} %copy-done, bf16[3,1024,1024]{2,1,0:T(8,128)(2,1)S(1)} %copy-done, ...), custom_call_target="tpu_custom_call", output_to_operand_aliasing={{0}: (4, {}), {1}: (5, {})} | custom-call | tf_op jit(solution)/shard_map/attend_forward/pallas_call | solution.py:335
  157.6 11.6 %mlp_up.1 = (bf16[512,4096]{1,0:T(8,128)(2,1)S(1)}, bf16[512,4096]{1,0:T(8,128)(2,1)}) custom-call(bf16[512,1024]{1,0:T(8,128)(2,1)S(1)} %add_convert_fusion.15.x_ref, bf16[1,256,4096]{2,1,0:T(8,128)(2,1)S(1)} %copy-done.9, bf16[1,256,4096]{2,1,0:T(8,128)(2,1)S(1)} %copy-done.28, bf16[1,256,4096]{2,1,0:T(8,128)(2,1)S(1)} %copy-done.30, ...), custom_call_target="tpu_custom_call" | custom-call | tf_op jit(solution)/shard_map/mlp_up/pallas_call | solution.py:509
  174.2 7.0 %weight_grads.4 = (bf16[1,256,4096]{2,1,0:T(8,128)(2,1)S(1)}, bf16[1,256,4096]{2,1,0:T(8,128)(2,1)S(1)}, bf16[1,256,4096]{2,1,0:T(8,128)(2,1)S(1)}, bf16[1,256,4096]{2,1,0:T(8,128)(2,1)S(1)}) custom-call(bf16[512,1024]{1,0:T(8,128)(2,1)S(1)} %copy-done.5, bf16[1,512,4096]{2,1,0:T(8,128)(2,1)S(1)} %bitcast.52), custom_call_target="tpu_custom_call" | custom-call | tf_op jit(solution)/shard_map/weight_grads/pallas_call | solution.py:560
  181.8 16.9 %collective-permute-done.25.refs_1_ = bf16[1,256,4096]{2,1,0:T(8,128)(2,1)S(1)} collective-permute-done((bf16[1,256,4096]{2,1,0:T(8,128)(2,1)S(1)}, bf16[1,256,4096]{2,1,0:T(8,128)(2,1)S(1)}, u32[]{:S(2)}, u32[]{:S(2)}) %collective-permute-start.25) | collective-permute-done | bytes 2097184 | tf_op jit(solution)/shard_map/ppermute | solution.py:37
  206.1 14.8 %mlp_down.1 = (bf16[512,4096]{1,0:T(8,128)(2,1)}, f32[1,4096]{1,0:T(1,128)S(1)}, f32[512,1024]{1,0:T(8,128)S(1)}) custom-call(bf16[512,1024]{1,0:T(8,128)(2,1)S(1)} %copy-done.5, bf16[1,256,4096]{2,1,0:T(8,128)(2,1)S(1)} %pad_maximum_fusion.2.refs_0_, bf16[1,256,4096]{2,1,0:T(8,128)(2,1)S(1)} %collective-permute-done.25.refs_1_, ...), custom_call_target="tpu_custom_call" | custom-call | tf_op jit(solution)/shard_map/mlp_down/pallas_call | solution.py:526
  223.0 7.9 %weight_grads.5 = (bf16[1,256,4096]{2,1,0:T(8,128)(2,1)S(1)}, bf16[1,256,4096]{2,1,0:T(8,128)(2,1)S(1)}, bf16[1,256,4096]{2,1,0:T(8,128)(2,1)S(1)}, bf16[1,256,4096]{2,1,0:T(8,128)(2,1)}) custom-call(bf16[512,1024]{1,0:T(8,128)(2,1)S(1)} %copy-done.15, bf16[1,512,4096]{2,1,0:T(8,128)(2,1)S(1)} %bitcast.55), custom_call_target="tpu_custom_call" | custom-call | tf_op jit(solution)/shard_map/weight_grads/pallas_call | solution.py:560
  251.3 4.5 %add_convert_fusion.3 = bf16[1,256,4096]{2,1,0:T(8,128)(2,1)} fusion(bf16[1,256,4096]{2,1,0:T(8,128)(2,1)} %collective-permute-done.32, bf16[1,256,4096]{2,1,0:T(8,128)(2,1)S(1)} %get-tuple-element.216), kind=kLoop, calls=%fused_computation.5 | loop fusion | flops 4194304 | bytes 6291456 | tf_op jit(solution)/shard_map/convert_element_type | solution.py:84
  259.0 5.0 %collective-permute-start.35 = (bf16[1,128,1024]{2,1,0:T(8,128)(2,1)S(1)}, bf16[1,128,1024]{2,1,0:T(8,128)(2,1)S(1)}, u32[]{:S(2)}, u32[]{:S(2)}) collective-permute-start(bf16[1,128,1024]{2,1,0:T(8,128)(2,1)S(1)} %get-tuple-element.373), channel_id=1, source_target_pairs={{0,1},{1,2},{2,3},{3,0},{4,5},{5,6},{6,7},{7,4},{8,9},{9,10},{10,1... | collective-permute-start | bytes 786440 | tf_op jit(solution)/shard_map/ppermute | solution.py:42
  267.3 21.5 %attend_backward.1.y_ref.grad_ref = bf16[3,1024,1024]{2,1,0:T(8,128)(2,1)S(1)} custom-call(s32[1,512]{1,0:T(1,128)S(1)} %bitcast.58, bf16[3,1024,1024]{2,1,0:T(8,128)(2,1)} %project.2.q_ref.k_ref.v_ref, bf16[3,1024,1024]{2,1,0:T(8,128)(2,1)} %project.2.q_ref.k_ref.v_ref, bf16[3,1024,1024]{2,1,0:T(8,128)(2,1)} %project.2.q_ref.k_ref.v_ref, ...), custom_call_target="tpu_custom_call" | custom-call | tf_op jit(solution)/shard_map/attend_backward/pallas_call | solution.py:359
  295.2 9.9 %weight_grads.7 = (bf16[4,256,1024]{2,1,0:T(8,128)(2,1)S(1)}, bf16[4,256,1024]{2,1,0:T(8,128)(2,1)S(1)}, bf16[4,256,1024]{2,1,0:T(8,128)(2,1)S(1)}, bf16[4,256,1024]{2,1,0:T(8,128)(2,1)S(1)}) custom-call(bf16[1024,1024]{1,0:T(8,128)(2,1)S(1)} %bitcast.51, ...), custom_call_target="tpu_custom_call", output_to_operand_aliasing={{0}: (2, {}), {1}: (3, {}), {2}: (4, {}), {3}: (5, {})} | custom-call | tf_op jit(solution)/shard_map/weight_grads/pallas_call | solution.py:560
  315.6 10.5 %project_back.1 = (f32[512,1024]{1,0:T(8,128)S(1)}, bf16[512,1024]{1,0:T(8,128)(2,1)S(1)}) custom-call(bf16[3,1024,1024]{2,1,0:T(8,128)(2,1)} %copy-done.1, bf16[4,256,1024]{2,1,0:T(8,128)(2,1)S(1)} %copy-done.4, bf16[4,256,1024]{2,1,0:T(8,128)(2,1)} %collective-permute-done.10.refs_1_, bf16[4,256,1024]{2,1,0:T(8,128)(2,1)} %collective-permute-done.11.refs_2_, ...), custom_call_target="tpu_custom_call" | custom-call | tf_op jit(solution)/shard_map/project_back/pallas_call | solution.py:447
  326.1 6.8 %collective-permute-done.42 = bf16[1,128,1024]{2,1,0:T(8,128)(2,1)S(1)} collective-permute-done((bf16[1,128,1024]{2,1,0:T(8,128)(2,1)S(1)}, bf16[1,128,1024]{2,1,0:T(8,128)(2,1)S(1)}, u32[]{:S(2)}, u32[]{:S(2)}) %collective-permute-start.42) | collective-permute-done | bytes 262176 | tf_op jit(solution)/shard_map/ppermute | solution.py:42
  333.0 4.9 %add_convert_fusion.1 = bf16[4,256,1024]{2,1,0:T(8,128)(2,1)} fusion(bf16[4,256,1024]{2,1,0:T(8,128)(2,1)} %collective-permute-done.39, bf16[4,256,1024]{2,1,0:T(8,128)(2,1)S(1)} %get-tuple-element.251), kind=kLoop, calls=%fused_computation.3 | loop fusion | flops 4194304 | bytes 6291456 | tf_op jit(solution)/shard_map/convert_element_type | solution.py:84
  353.0 11.1 %mlp_out.1 = f32[512,1024]{1,0:T(8,128)} custom-call(s32[8]{0:T(128)S(1)} %copy-done.51, bf16[512,4096]{1,0:T(8,128)(2,1)} %copy-done.13, bf16[1,256,4096]{2,1,0:T(8,128)(2,1)S(1)} %copy-done.12, bf16[1,256,4096]{2,1,0:T(8,128)(2,1)S(1)} %copy-done.34, bf16[1,256,4096]{2,1,0:T(8,128)(2,1)S(1)} %copy-done.37, bf16[1,256,4096]{2,1,0:T(8,128)(2,1)S(1)} %copy-done.39, ...), custom_call_target="tpu_custom_call" | custom-call | tf_op jit(solution)/shard_map/mlp_out/pallas_call | solution.py:603
  364.2 6.3 %collective-permute-done.45 = bf16[512,1024]{1,0:T(8,128)(2,1)} collective-permute-done((bf16[512,1024]{1,0:T(8,128)(2,1)}, bf16[512,1024]{1,0:T(8,128)(2,1)}, u32[]{:S(2)}, u32[]{:S(2)}) %collective-permute-start.45) | collective-permute-done | bytes 1048608 | tf_op jit(solution)/shard_map/ppermute | solution.py:804
  411.7 5.2 %collective-permute-done.55 = bf16[4,128,256]{2,1,0:T(8,128)(2,1)S(1)} collective-permute-done((bf16[4,128,256]{2,1,0:T(8,128)(2,1)S(1)}, bf16[4,128,256]{2,1,0:T(8,128)(2,1)S(1)}, u32[]{:S(2)}, u32[]{:S(2)}) %collective-permute-start.55) | collective-permute-done | bytes 262176 | tf_op jit(solution)/shard_map/ppermute | solution.py:42
  416.9 16.0 %collective-permute-done.54 = bf16[4,128,256]{2,1,0:T(8,128)(2,1)S(1)} collective-permute-done((bf16[4,128,256]{2,1,0:T(8,128)(2,1)S(1)}, bf16[4,128,256]{2,1,0:T(8,128)(2,1)S(1)}, u32[]{:S(2)}, u32[]{:S(2)}) %collective-permute-start.54) | collective-permute-done | bytes 262176 | tf_op jit(solution)/shard_map/ppermute | solution.py:42
  (391 shorter events, 196.3 us)
Async XLA Ops:
  2.5 23.1 %collective-permute-start = (bf16[4,128,256]{2,1,0:T(8,128)(2,1)S(1)}, bf16[4,128,256]{2,1,0:T(8,128)(2,1)S(1)}, u32[]{:S(2)}, u32[]{:S(2)}) collective-permute-start(bf16[4,128,256]{2,1,0:T(8,128)(2,1)S(1)} %pad_maximum_fusion.6), channel_id=1, source_target_pairs={{0,1},{1,2},{2,3},{3,0},{4,5},{5,6},{6,7},{7,4},{8,9},{9,10},{10,1... | collective-permute-start | bytes 786440 | tf_op jit(solution)/shard_map/ppermute | solution.py:42
  41.0 32.3 %collective-permute-start.10 = (bf16[4,256,1024]{2,1,0:T(8,128)(2,1)S(1)}, bf16[4,256,1024]{2,1,0:T(8,128)(2,1)}, u32[]{:S(2)}, u32[]{:S(2)}) collective-permute-start(bf16[4,256,1024]{2,1,0:T(8,128)(2,1)S(1)} %pad_maximum_fusion.refs_0_), channel_id=1, source_target_pairs={{0,16},{4,12},{8,24},{12,4},{16,0},{20,28},{24,8},{28,20},{1,17},{... | collective-permute-start | bytes 6291464 | tf_op jit(solution)/shard_map/ppermute | solution.py:37
  42.3 31.1 %collective-permute-start.11 = (bf16[4,256,1024]{2,1,0:T(8,128)(2,1)S(1)}, bf16[4,256,1024]{2,1,0:T(8,128)(2,1)}, u32[]{:S(2)}, u32[]{:S(2)}) collective-permute-start(bf16[4,256,1024]{2,1,0:T(8,128)(2,1)S(1)} %pad_maximum_fusion.refs_0_), channel_id=1, source_target_pairs={{0,4},{4,0},{8,12},{12,8},{16,20},{20,16},{24,28},{28,24},{1,5},{5... | collective-permute-start | bytes 6291464 | tf_op jit(solution)/shard_map/ppermute | solution.py:31
  42.3 31.1 %collective-permute-start.12 = (bf16[512,1024]{1,0:T(8,128)(2,1)S(1)}, bf16[512,1024]{1,0:T(8,128)(2,1)}, u32[]{:S(2)}, u32[]{:S(2)}) collective-permute-start(bf16[512,1024]{1,0:T(8,128)(2,1)S(1)} %copy-done.53), channel_id=1, source_target_pairs={{0,1},{1,2},{2,3},{4,5},{5,6},{6,7},{8,9},{9,10},{10,11},{12,13},{... | collective-permute-start | bytes 3145736 | tf_op jit(solution)/shard_map/ppermute | solution.py:710
  73.4 22.6 %collective-permute-start.13 = (bf16[1,128,1024]{2,1,0:T(8,128)(2,1)}, bf16[1,128,1024]{2,1,0:T(8,128)(2,1)}, u32[]{:S(2)}, u32[]{:S(2)}) collective-permute-start(bf16[1,128,1024]{2,1,0:T(8,128)(2,1)} %bitcast.67), channel_id=1, source_target_pairs={{0,1},{1,2},{2,3},{3,0},{4,5},{5,6},{6,7},{7,4},{8,9},{9,10},{10,1... | collective-permute-start | bytes 786440 | tf_op jit(solution)/shard_map/ppermute | solution.py:42
  115.8 26.5 %collective-permute-start.18 = (bf16[1,256,4096]{2,1,0:T(8,128)(2,1)S(1)}, bf16[1,256,4096]{2,1,0:T(8,128)(2,1)S(1)}, u32[]{:S(2)}, u32[]{:S(2)}) collective-permute-start(bf16[1,256,4096]{2,1,0:T(8,128)(2,1)S(1)} %pad_maximum_fusion.1.refs_0_.refs_5_), channel_id=1, source_target_pairs={{0,16},{4,12},{8,24},{12,4},{16,0},{20,28},{24,8},{28,20},{1,17},{... | collective-permute-start | bytes 6291464 | tf_op jit(solution)/shard_map/ppermute | solution.py:37
  116.3 25.9 %collective-permute-start.19 = (bf16[1,256,4096]{2,1,0:T(8,128)(2,1)S(1)}, bf16[1,256,4096]{2,1,0:T(8,128)(2,1)S(1)}, u32[]{:S(2)}, u32[]{:S(2)}) collective-permute-start(bf16[1,256,4096]{2,1,0:T(8,128)(2,1)S(1)} %pad_maximum_fusion.1.refs_0_.refs_5_), channel_id=1, source_target_pairs={{0,4},{4,0},{8,12},{12,8},{16,20},{20,16},{24,28},{28,24},{1,5},{5... | collective-permute-start | bytes 6291464 | tf_op jit(solution)/shard_map/ppermute | solution.py:31
  116.3 25.8 %collective-permute-start.20 = (bf16[1,128,1024]{2,1,0:T(8,128)(2,1)S(1)}, bf16[1,128,1024]{2,1,0:T(8,128)(2,1)S(1)}, u32[]{:S(2)}, u32[]{:S(2)}) collective-permute-start(bf16[1,128,1024]{2,1,0:T(8,128)(2,1)S(1)} %bitcast.60), channel_id=1, source_target_pairs={{0,1},{1,2},{2,3},{3,0},{4,5},{5,6},{6,7},{7,4},{8,9},{9,10},{10,1... | collective-permute-start | bytes 786440 | tf_op jit(solution)/shard_map/ppermute | solution.py:42
  172.6 26.1 %collective-permute-start.25 = (bf16[1,256,4096]{2,1,0:T(8,128)(2,1)S(1)}, bf16[1,256,4096]{2,1,0:T(8,128)(2,1)S(1)}, u32[]{:S(2)}, u32[]{:S(2)}) collective-permute-start(bf16[1,256,4096]{2,1,0:T(8,128)(2,1)S(1)} %pad_maximum_fusion.2.refs_0_), channel_id=1, source_target_pairs={{0,16},{4,12},{8,24},{12,4},{16,0},{20,28},{24,8},{28,20},{1,17},{... | collective-permute-start | bytes 6291464 | tf_op jit(solution)/shard_map/ppermute | solution.py:37
  174.2 24.5 %collective-permute-start.26 = (bf16[1,256,4096]{2,1,0:T(8,128)(2,1)S(1)}, bf16[1,256,4096]{2,1,0:T(8,128)(2,1)S(1)}, u32[]{:S(2)}, u32[]{:S(2)}) collective-permute-start(bf16[1,256,4096]{2,1,0:T(8,128)(2,1)S(1)} %pad_maximum_fusion.2.refs_0_), channel_id=1, source_target_pairs={{0,4},{4,0},{8,12},{12,8},{16,20},{20,16},{24,28},{28,24},{1,5},{5... | collective-permute-start | bytes 6291464 | tf_op jit(solution)/shard_map/ppermute | solution.py:31
  202.9 28.0 %collective-permute-start.30 = (bf16[1,256,4096]{2,1,0:T(8,128)(2,1)}, bf16[1,256,4096]{2,1,0:T(8,128)(2,1)}, u32[]{:S(2)}, u32[]{:S(2)}) collective-permute-start(bf16[1,256,4096]{2,1,0:T(8,128)(2,1)} %add_convert_fusion.5), channel_id=1, source_target_pairs={{0,16},{4,12},{8,24},{12,4},{16,0},{20,28},{24,8},{28,20},{1,17},{... | collective-permute-start | bytes 6291464 | tf_op jit(solution)/shard_map/ppermute | solution.py:37
  231.0 20.3 %collective-permute-start.32 = (bf16[1,256,4096]{2,1,0:T(8,128)(2,1)}, bf16[1,256,4096]{2,1,0:T(8,128)(2,1)}, u32[]{:S(2)}, u32[]{:S(2)}) collective-permute-start(bf16[1,256,4096]{2,1,0:T(8,128)(2,1)} %get-tuple-element.225), channel_id=1, source_target_pairs={{0,4},{4,0},{8,12},{12,8},{16,20},{20,16},{24,28},{28,24},{1,5},{5... | collective-permute-start | bytes 6291464 | tf_op jit(solution)/shard_map/ppermute | solution.py:31
  255.8 33.1 %collective-permute-start.34 = (bf16[1,256,4096]{2,1,0:T(8,128)(2,1)}, bf16[1,256,4096]{2,1,0:T(8,128)(2,1)}, u32[]{:S(2)}, u32[]{:S(2)}) collective-permute-start(bf16[1,256,4096]{2,1,0:T(8,128)(2,1)} %add_convert_fusion.3), channel_id=1, source_target_pairs={{0,16},{4,12},{8,24},{12,4},{16,0},{20,28},{24,8},{28,20},{1,17},{... | collective-permute-start | bytes 6291464 | tf_op jit(solution)/shard_map/ppermute | solution.py:37
  259.0 29.8 %collective-permute-start.35 = (bf16[1,128,1024]{2,1,0:T(8,128)(2,1)S(1)}, bf16[1,128,1024]{2,1,0:T(8,128)(2,1)S(1)}, u32[]{:S(2)}, u32[]{:S(2)}) collective-permute-start(bf16[1,128,1024]{2,1,0:T(8,128)(2,1)S(1)} %get-tuple-element.373), channel_id=1, source_target_pairs={{0,1},{1,2},{2,3},{3,0},{4,5},{5,6},{6,7},{7,4},{8,9},{9,10},{10,1... | collective-permute-start | bytes 786440 | tf_op jit(solution)/shard_map/ppermute | solution.py:42
  264.0 24.8 %collective-permute-start.36 = (bf16[1,128,1024]{2,1,0:T(8,128)(2,1)S(1)}, bf16[1,128,1024]{2,1,0:T(8,128)(2,1)S(1)}, u32[]{:S(2)}, u32[]{:S(2)}) collective-permute-start(bf16[1,128,1024]{2,1,0:T(8,128)(2,1)S(1)} %get-tuple-element.372), channel_id=1, source_target_pairs={{0,2},{1,3},{2,0},{3,1},{4,6},{5,7},{6,4},{7,5},{8,10},{9,11},{10,... | collective-permute-start | bytes 786440 | tf_op jit(solution)/shard_map/ppermute | solution.py:42
  266.2 22.6 %collective-permute-start.37 = (bf16[1,128,1024]{2,1,0:T(8,128)(2,1)S(1)}, bf16[1,128,1024]{2,1,0:T(8,128)(2,1)S(1)}, u32[]{:S(2)}, u32[]{:S(2)}) collective-permute-start(bf16[1,128,1024]{2,1,0:T(8,128)(2,1)S(1)} %get-tuple-element.370), channel_id=1, source_target_pairs={{0,3},{1,0},{2,1},{3,2},{4,7},{5,4},{6,5},{7,6},{8,11},{9,8},{10,9... | collective-permute-start | bytes 786440 | tf_op jit(solution)/shard_map/ppermute | solution.py:42
  309.0 23.9 %collective-permute-start.39 = (bf16[4,256,1024]{2,1,0:T(8,128)(2,1)S(1)}, bf16[4,256,1024]{2,1,0:T(8,128)(2,1)}, u32[]{:S(2)}, u32[]{:S(2)}) collective-permute-start(bf16[4,256,1024]{2,1,0:T(8,128)(2,1)S(1)} %get-tuple-element.243), channel_id=1, source_target_pairs={{0,4},{4,0},{8,12},{12,8},{16,20},{20,16},{24,28},{28,24},{1,5},{5... | collective-permute-start | bytes 6291464 | tf_op jit(solution)/shard_map/ppermute | solution.py:31
  309.0 23.9 %collective-permute-start.40 = (bf16[4,256,1024]{2,1,0:T(8,128)(2,1)S(1)}, bf16[4,256,1024]{2,1,0:T(8,128)(2,1)S(1)}, u32[]{:S(2)}, u32[]{:S(2)}) collective-permute-start(bf16[4,256,1024]{2,1,0:T(8,128)(2,1)S(1)} %get-tuple-element.244), channel_id=1, source_target_pairs={{0,4},{4,0},{8,12},{12,8},{16,20},{20,16},{24,28},{28,24},{1,5},{5... | collective-permute-start | bytes 6291464 | tf_op jit(solution)/shard_map/ppermute | solution.py:31
  312.6 20.3 %collective-permute-start.42 = (bf16[1,128,1024]{2,1,0:T(8,128)(2,1)S(1)}, bf16[1,128,1024]{2,1,0:T(8,128)(2,1)S(1)}, u32[]{:S(2)}, u32[]{:S(2)}) collective-permute-start(bf16[1,128,1024]{2,1,0:T(8,128)(2,1)S(1)} %get-tuple-element.368), channel_id=1, source_target_pairs={{0,2},{1,3},{2,0},{3,1},{4,6},{5,7},{6,4},{7,5},{8,10},{9,11},{10,... | collective-permute-start | bytes 786440 | tf_op jit(solution)/shard_map/ppermute | solution.py:42
  337.9 32.6 %collective-permute-start.44 = (bf16[4,256,1024]{2,1,0:T(8,128)(2,1)}, bf16[4,256,1024]{2,1,0:T(8,128)(2,1)}, u32[]{:S(2)}, u32[]{:S(2)}) collective-permute-start(bf16[4,256,1024]{2,1,0:T(8,128)(2,1)} %add_convert_fusion.1), channel_id=1, source_target_pairs={{0,16},{4,12},{8,24},{12,4},{16,0},{20,28},{24,8},{28,20},{1,17},{... | collective-permute-start | bytes 6291464 | tf_op jit(solution)/shard_map/ppermute | solution.py:37
  339.4 31.1 %collective-permute-start.45 = (bf16[512,1024]{1,0:T(8,128)(2,1)}, bf16[512,1024]{1,0:T(8,128)(2,1)}, u32[]{:S(2)}, u32[]{:S(2)}) collective-permute-start(bf16[512,1024]{1,0:T(8,128)(2,1)} %copy-done.52), channel_id=1, source_target_pairs={{1,0},{2,1},{3,2},{5,4},{6,5},{7,6},{9,8},{10,9},{11,10},{13,12},{... | collective-permute-start | bytes 3145736 | tf_op jit(solution)/shard_map/ppermute | solution.py:804
  374.9 30.2 %collective-permute-start.46 = (bf16[4,128,1024]{2,1,0:T(8,128)(2,1)}, bf16[4,128,1024]{2,1,0:T(8,128)(2,1)}, u32[]{:S(2)}, u32[]{:S(2)}) collective-permute-start(bf16[4,128,1024]{2,1,0:T(8,128)(2,1)} %add_convert_fusion.8), channel_id=1, source_target_pairs={{0,8},{4,20},{8,0},{12,28},{16,24},{20,4},{24,16},{28,12},{1,9},{5... | collective-permute-start | bytes 3145736 | tf_op jit(solution)/shard_map/ppermute | solution.py:37
  410.1 22.8 %collective-permute-start.54 = (bf16[4,128,256]{2,1,0:T(8,128)(2,1)S(1)}, bf16[4,128,256]{2,1,0:T(8,128)(2,1)S(1)}, u32[]{:S(2)}, u32[]{:S(2)}) collective-permute-start(bf16[4,128,256]{2,1,0:T(8,128)(2,1)S(1)} %get-tuple-element.363), channel_id=1, source_target_pairs={{0,2},{1,3},{2,0},{3,1},{4,6},{5,7},{6,4},{7,5},{8,10},{9,11},{10,... | collective-permute-start | bytes 786440 | tf_op jit(solution)/shard_map/ppermute | solution.py:42
  410.4 22.5 %collective-permute-start.53 = (bf16[4,128,256]{2,1,0:T(8,128)(2,1)S(1)}, bf16[4,128,256]{2,1,0:T(8,128)(2,1)S(1)}, u32[]{:S(2)}, u32[]{:S(2)}) collective-permute-start(bf16[4,128,256]{2,1,0:T(8,128)(2,1)S(1)} %get-tuple-element.362), channel_id=1, source_target_pairs={{0,1},{1,2},{2,3},{3,0},{4,5},{5,6},{6,7},{7,4},{8,9},{9,10},{10,1... | collective-permute-start | bytes 786440 | tf_op jit(solution)/shard_map/ppermute | solution.py:42
  (115 other events, 1119.0 us)
